TPU v7x, 32 devices: a whole 2x2x4 slice. The times are simulated.
32 devices in a mesh: groups: 2 (over y), dp: 4 (over z), tensor: 4 (over x, core).
Axes of the slice: x: 2, y: 2, z: 4, core: 2. Of those that a mesh axis runs over, the one named last changes fastest.
Arguments:
- ssm_input: bfloat16 [8, 512, 8192], P(('groups', 'dp'), None, 'tensor'), parts along dimension 0, may hold values from -6 to 6
- input_proj: bfloat16 [8, 512, 512], P(('groups', 'dp'), None, 'tensor'), parts along dimension 0, may hold values from -2 to 2
- output_proj: bfloat16 [8, 512, 512], P(('groups', 'dp'), None, 'tensor'), parts along dimension 0, may hold values from -2 to 2
- step_raw: float32 [8, 128, 512], P(('groups', 'dp'), 'tensor'), parts along dimension 0, may hold values from -4 to 4
- step_bias: float32 [128], P('tensor'), may hold values from -1 to 1
- decay_log: float32 [128], P('tensor'), may hold values from -5.8 to -2.8
- skip_gain: float32 [128], P('tensor'), may hold values from 0.5 to 1.5
- norm_gain: float32 [8192], P('tensor'), may hold values from 0.1 to 1.9
- cache_states: bfloat16 [32, 128, 64, 128], P('groups', 'tensor', 'dp'), parts along dimension 0, may hold values from -6 to 6
- slot_decay: float32 [32, 128], P('groups', 'tensor'), parts along dimension 0, may hold values from 0.2 to 0.9
- template_state: bfloat16 [256, 64, 128], P(('groups', 'tensor'), 'dp'), parts along dimension 0, may hold values from -6 to 6
- slot_ids: int32 [8], P(('groups', 'dp')), parts along dimension 0, may hold values from 0 to 15
- row_lengths: int32 [8], P(('groups', 'dp')), parts along dimension 0, may hold values from 256 to 512
- row_offsets: int32 [8], P(('groups', 'dp')), parts along dimension 0, may hold values from 0 to 127
Outputs:
- mixed: bfloat16 [8, 512, 8192], P(('groups', 'dp'), None, 'tensor'), parts along dimension 0
- new_states: bfloat16 [8, 128, 64, 128], P('groups', 'tensor', 'dp'), parts along dimension 0
There are 2 independent parts, one for each index of `groups`. A program takes and returns all parts, laid end to end along the dimension named above; an argument that names none is the same for every part. Nothing has to cross between parts.
All inputs are finite; a program needn't handle non-finite values.
Results may differ from a plain program's by a relative error of at most 0.0049.
Values may be sent and summed in bfloat16 or wider, within the bound.
No kernel may reach another device: no remote copies, remote signals or barrier semaphores. Data moves between devices by JAX's collectives and lax.ppermute only.
A program may use at most 64 MiB of HBM per device.

v0:
```python
import math

import jax
import jax.numpy as jnp
from jax import lax
from jax.sharding import PartitionSpec as P

HEAD_SIZE = 64
GROUP_HEADS = 32


def lookup_decay(wanted, slot_decay):
    picked = (wanted[:, None] == jnp.arange(slot_decay.shape[0], dtype=jnp.int32)[None, :]).astype(
        jnp.float32
    )
    return jnp.dot(picked, slot_decay, precision=lax.Precision.HIGHEST)


def local(
    ssm_input,
    input_proj,
    output_proj,
    step_raw,
    step_bias,
    decay_log,
    skip_gain,
    norm_gain,
    cache_states,
    slot_decay,
    template_state,
    slot_ids,
    row_lengths,
    row_offsets,
):
    rows_here = ssm_input.shape[0]
    length = ssm_input.shape[1]
    heads_here = step_raw.shape[1]
    every_slot = lax.all_gather(slot_ids, "dp", axis=0, tiled=True)
    persona = lax.all_to_all(
        cache_states[every_slot], "dp", split_axis=0, concat_axis=2, tiled=True
    )
    whole_template = lax.all_gather(template_state, "dp", axis=1, tiled=True)
    factor = lookup_decay(slot_ids, slot_decay)
    resumed = (
        persona.astype(jnp.float32)
        + factor[:, :, None, None] * whole_template.astype(jnp.float32)[None]
    ).astype(jnp.bfloat16)
    position = jnp.arange(length, dtype=jnp.int32)
    causal = position[:, None] >= position[None, :]
    alive_mask = position[None, :] < row_lengths[:, None]
    step_size = jnp.where(
        alive_mask[:, None, :], jax.nn.softplus(step_raw + step_bias[None, :, None]), 0.0
    )
    logdecay = jnp.cumsum(-jnp.exp(decay_log)[None, :, None] * step_size, axis=2)
    gram = jnp.einsum("rsn,run->rsu", output_proj, input_proj, preferred_element_type=jnp.float32)
    heads_x = ssm_input.reshape(rows_here, length, heads_here, HEAD_SIZE)
    block = math.gcd(heads_here, 4)
    nblocks = heads_here // block
    decay_blocks = jnp.transpose(logdecay.reshape(rows_here, nblocks, block, length), (1, 0, 2, 3))
    step_blocks = jnp.transpose(step_size.reshape(rows_here, nblocks, block, length), (1, 0, 2, 3))
    value_blocks = jnp.transpose(
        heads_x.reshape(rows_here, length, nblocks, block, HEAD_SIZE), (2, 0, 1, 3, 4)
    )

    def intra_block(items):
        decay_part, step_part, value_part = items
        spread = jnp.where(
            causal[None, None], decay_part[:, :, :, None] - decay_part[:, :, None, :], 0.0
        )
        weights = jnp.where(
            causal[None, None], gram[:, None] * jnp.exp(spread) * step_part[:, :, None, :], 0.0
        ).astype(jnp.bfloat16)
        return jnp.einsum(
            "rhsu,ruhp->rshp", weights, value_part, preferred_element_type=jnp.float32
        )

    intra_parts = lax.map(intra_block, (decay_blocks, step_blocks, value_blocks))
    intra = jnp.transpose(intra_parts, (1, 2, 0, 3, 4)).reshape(
        rows_here, length, heads_here, HEAD_SIZE
    )
    tail = jnp.exp(logdecay[:, :, -1:] - logdecay) * step_size
    carry = (jnp.swapaxes(tail, 1, 2)[..., None] * heads_x.astype(jnp.float32)).astype(jnp.bfloat16)
    local_state = jnp.einsum(
        "ruhp,run->rhpn", carry, input_proj, preferred_element_type=jnp.float32
    )
    carried = jnp.einsum("rsn,rhpn->rshp", output_proj, resumed, preferred_element_type=jnp.float32)
    carried = carried * jnp.exp(jnp.swapaxes(logdecay, 1, 2))[..., None]
    scan = intra + carried + skip_gain[None, None, :, None] * heads_x.astype(jnp.float32)
    grouped = scan.reshape(rows_here, length, heads_here // GROUP_HEADS, GROUP_HEADS * HEAD_SIZE)
    meansq = jnp.mean(grouped * grouped, axis=-1, keepdims=True)
    normed = (grouped * lax.rsqrt(meansq + 1e-05)).reshape(
        rows_here, length, heads_here * HEAD_SIZE
    ) * norm_gain
    keep_mask = alive_mask & (position[None, :] >= row_offsets[:, None])
    mixed = jnp.where(keep_mask[:, :, None], normed, 0.0).astype(jnp.bfloat16)
    final_state = (
        local_state + jnp.exp(logdecay[:, :, -1])[:, :, None, None] * resumed.astype(jnp.float32)
    ).astype(jnp.bfloat16)
    new_states = lax.all_to_all(final_state, "dp", split_axis=2, concat_axis=0, tiled=True)
    return (mixed, new_states)


def solution(mesh):
    return jax.shard_map(
        local,
        mesh=mesh,
        in_specs=(
            P(("groups", "dp"), None, "tensor"),
            P(("groups", "dp"), None, "tensor"),
            P(("groups", "dp"), None, "tensor"),
            P(("groups", "dp"), "tensor", None),
            P("tensor"),
            P("tensor"),
            P("tensor"),
            P("tensor"),
            P("groups", "tensor", "dp", None),
            P("groups", "tensor"),
            P(("groups", "tensor"), "dp", None),
            P(("groups", "dp")),
            P(("groups", "dp")),
            P(("groups", "dp")),
        ),
        out_specs=(P(("groups", "dp"), None, "tensor"), P("groups", "tensor", "dp", None)),
        check_vma=False,
    )
```

profile of v0, /device:TPU:0, one launch (start us, length us, event | category | flops | bytes accessed | tf_op | source)
XLA Modules:
  0.0 108.3 jit_solution(7587526512008407589)
XLA Ops:
  0.6 0.0 copy-start
  0.6 0.0 copy-start.3
  0.7 0.0 copy-start.2
  1.5 1.2 %dynamic-slice = u32[1]{0:T(128)} dynamic-slice(u32[32]{0:T(128)} %constant.41, u32[]{:T(128)S(6)} %add.56), dynamic_slice_sizes={1} | dynamic-slice | bytes 12
  2.7 0.8 dynamic-update-slice
  3.5 9.9 %all-reduce = s32[4]{0:T(128)S(1)} all-reduce(s32[4]{0:T(128)S(1)} %dynamic-update-slice), channel_id=1, replica_groups=mesh['groups'=2,'dp'=4,'tensor'=4] {'dp'}, use_global_device_ids=true, to_apply=%add | all-reduce | flops 4 | bytes 32
  13.4 0.0 copy-done
  13.4 1.4 %gather_fusion = bf16[4,32,16,128]{3,2,1,0:T(8,128)(2,1)} fusion(bf16[16,32,16,128]{3,2,1,0:T(8,128)(2,1)S(1)} %copy-done, s32[1024]{0:T(1024)S(1)} %pad_clamp_fusion), kind=kCustom, calls=%fused_computation | custom fusion | bytes 1048592 | tf_op jit(solution)/shard_map/gather | solution.py:40
  14.8 3.5 %all-to-all-start = ((bf16[4,32,16,128]{3,2,1,0:T(8,128)(2,1)}), bf16[4,32,16,128]{3,2,1,0:T(8,128)(2,1)S(1)}, u32[]{:S(2)}, u32[]{:S(2)}) async-start(bf16[4,32,16,128]{3,2,1,0:T(8,128)(2,1)} %gather_fusion), calls=%async_computation | async-start | bytes 1048576 | tf_op jit(solution)/shard_map/all_to_all | solution.py:39
  18.9 0.7 exponential_negate_fusion
  19.6 1.0 multiply_bitcast_fusion.1
  20.6 1.2 %reduce-window.6 = f32[1,32,4,128]{3,1,2,0:T(8,128)S(1)} reduce-window(f32[1,32,4,128]{3,1,2,0:T(8,128)S(1)} %bitcast.123, f32[]{:T(128)} %constant.17.clone.1), window={size=1x1x1x128 pad=0_0x0_0x0_0x127_0}, to_apply=%region_0.1 | reduce-window | flops 2080768 | bytes 131076 | tf_op jit(solution)/shard_map/reduce-window
  21.8 0.2 slice_reduce_fusion
  22.0 0.1 copy.53
  22.1 3.9 %copy.50 = bf16[1,512,2048]{1,2,0:T(8,128)(2,1)} copy(bf16[1,512,2048]{2,1,0:T(8,128)(2,1)} %param.16) | data formatting | bytes 4194304 | tf_op args[0]
  26.1 0.1 broadcast.185
  26.2 0.1 reduce_window_sum.34
  26.3 0.0 copy-done.3
  26.3 0.0 copy-done.2
  26.3 1.3 %convolution_bitcast_fusion = f32[1,512,512]{2,1,0:T(8,128)} fusion(bf16[1,512,128]{2,1,0:T(8,128)(2,1)S(1)} %copy-done.3, bf16[1,512,128]{2,1,0:T(8,128)(2,1)S(1)} %copy-done.2), kind=kOutput, calls=%fused_computation.23 | convolution fusion | flops 67108864 | bytes 1310720 | tf_op jit(solution)/shard_map/rsn,run->rsu/dot_general | solution.py:55
  27.6 28.7 %while.12 = (s32[]{:T(128)}, f32[8,1,512,4,64]{2,4,3,1,0:T(8,128)}, bf16[8,1,512,4,64]{2,4,3,1,0:T(8,128)(2,1)}, f32[1,512,512]{2,1,0:T(8,128)}, f32[8,1,4,512]{...) while((s32[]{:T(128)}, f32[8,1,512,4,64]{2,4,3,1,0:T(8,128)}, ...), condition=%wide.region_3.4_spmd.clone.clone, body=%wide.region_2.3_spmd.clone.clone.sunk | while | flops 140771328 | bytes 2434133 | solution.py:77
  27.6 0.1 iota_compare_fusion.4
  27.7 3.5 %fusion.31 = f32[8,1,512,4,64]{2,4,3,1,0:T(8,128)} fusion(f32[8,1,512,4,64]{2,4,3,1,0:T(8,128)} %get-tuple-element.162, s32[]{:T(128)} %get-tuple-element.161, f32[4,512]{1,0:T(4,128)S(1)} %get-tuple-element.152, f32[4,512]{1,0:T(4,128)S(1)} %get-tuple-element.153, f32[512,512]{1,0:T(8,128)} %bitcast.118, ...), kind=kOutput, calls=%fused_computation.6.clone.1 | convolution fusion | flops 140509184 | bytes 2122752 | tf_op jit(solution)/shard_map/while/body/eval_jaxpr/rhsu,ruhp->rshp/dot_general | solution.py:73
  31.2 0.1 iota_compare_fusion.4
  31.2 3.5 %fusion.31 = f32[8,1,512,4,64]{2,4,3,1,0:T(8,128)} fusion(f32[8,1,512,4,64]{2,4,3,1,0:T(8,128)} %get-tuple-element.162, s32[]{:T(128)} %get-tuple-element.161, f32[4,512]{1,0:T(4,128)S(1)} %get-tuple-element.152, f32[4,512]{1,0:T(4,128)S(1)} %get-tuple-element.153, f32[512,512]{1,0:T(8,128)} %bitcast.118, ...), kind=kOutput, calls=%fused_computation.6.clone.1 | convolution fusion | flops 140509184 | bytes 2122752 | tf_op jit(solution)/shard_map/while/body/eval_jaxpr/rhsu,ruhp->rshp/dot_general | solution.py:73
  34.7 0.1 iota_compare_fusion.4
  34.8 3.5 %fusion.31 = f32[8,1,512,4,64]{2,4,3,1,0:T(8,128)} fusion(f32[8,1,512,4,64]{2,4,3,1,0:T(8,128)} %get-tuple-element.162, s32[]{:T(128)} %get-tuple-element.161, f32[4,512]{1,0:T(4,128)S(1)} %get-tuple-element.152, f32[4,512]{1,0:T(4,128)S(1)} %get-tuple-element.153, f32[512,512]{1,0:T(8,128)} %bitcast.118, ...), kind=kOutput, calls=%fused_computation.6.clone.1 | convolution fusion | flops 140509184 | bytes 2122752 | tf_op jit(solution)/shard_map/while/body/eval_jaxpr/rhsu,ruhp->rshp/dot_general | solution.py:73
  38.4 0.1 iota_compare_fusion.4
  38.4 3.5 %fusion.31 = f32[8,1,512,4,64]{2,4,3,1,0:T(8,128)} fusion(f32[8,1,512,4,64]{2,4,3,1,0:T(8,128)} %get-tuple-element.162, s32[]{:T(128)} %get-tuple-element.161, f32[4,512]{1,0:T(4,128)S(1)} %get-tuple-element.152, f32[4,512]{1,0:T(4,128)S(1)} %get-tuple-element.153, f32[512,512]{1,0:T(8,128)} %bitcast.118, ...), kind=kOutput, calls=%fused_computation.6.clone.1 | convolution fusion | flops 140509184 | bytes 2122752 | tf_op jit(solution)/shard_map/while/body/eval_jaxpr/rhsu,ruhp->rshp/dot_general | solution.py:73
  41.9 0.1 iota_compare_fusion.4
  42.0 3.5 %fusion.31 = f32[8,1,512,4,64]{2,4,3,1,0:T(8,128)} fusion(f32[8,1,512,4,64]{2,4,3,1,0:T(8,128)} %get-tuple-element.162, s32[]{:T(128)} %get-tuple-element.161, f32[4,512]{1,0:T(4,128)S(1)} %get-tuple-element.152, f32[4,512]{1,0:T(4,128)S(1)} %get-tuple-element.153, f32[512,512]{1,0:T(8,128)} %bitcast.118, ...), kind=kOutput, calls=%fused_computation.6.clone.1 | convolution fusion | flops 140509184 | bytes 2122752 | tf_op jit(solution)/shard_map/while/body/eval_jaxpr/rhsu,ruhp->rshp/dot_general | solution.py:73
  45.5 0.1 iota_compare_fusion.4
  45.6 3.5 %fusion.31 = f32[8,1,512,4,64]{2,4,3,1,0:T(8,128)} fusion(f32[8,1,512,4,64]{2,4,3,1,0:T(8,128)} %get-tuple-element.162, s32[]{:T(128)} %get-tuple-element.161, f32[4,512]{1,0:T(4,128)S(1)} %get-tuple-element.152, f32[4,512]{1,0:T(4,128)S(1)} %get-tuple-element.153, f32[512,512]{1,0:T(8,128)} %bitcast.118, ...), kind=kOutput, calls=%fused_computation.6.clone.1 | convolution fusion | flops 140509184 | bytes 2122752 | tf_op jit(solution)/shard_map/while/body/eval_jaxpr/rhsu,ruhp->rshp/dot_general | solution.py:73
  49.1 0.1 iota_compare_fusion.4
  49.2 3.5 %fusion.31 = f32[8,1,512,4,64]{2,4,3,1,0:T(8,128)} fusion(f32[8,1,512,4,64]{2,4,3,1,0:T(8,128)} %get-tuple-element.162, s32[]{:T(128)} %get-tuple-element.161, f32[4,512]{1,0:T(4,128)S(1)} %get-tuple-element.152, f32[4,512]{1,0:T(4,128)S(1)} %get-tuple-element.153, f32[512,512]{1,0:T(8,128)} %bitcast.118, ...), kind=kOutput, calls=%fused_computation.6.clone.1 | convolution fusion | flops 140509184 | bytes 2122752 | tf_op jit(solution)/shard_map/while/body/eval_jaxpr/rhsu,ruhp->rshp/dot_general | solution.py:73
  52.7 0.1 iota_compare_fusion.4
  52.8 3.5 %fusion.31 = f32[8,1,512,4,64]{2,4,3,1,0:T(8,128)} fusion(f32[8,1,512,4,64]{2,4,3,1,0:T(8,128)} %get-tuple-element.162, s32[]{:T(128)} %get-tuple-element.161, f32[4,512]{1,0:T(4,128)S(1)} %get-tuple-element.152, f32[4,512]{1,0:T(4,128)S(1)} %get-tuple-element.153, f32[512,512]{1,0:T(8,128)} %bitcast.118, ...), kind=kOutput, calls=%fused_computation.6.clone.1 | convolution fusion | flops 140509184 | bytes 2122752 | tf_op jit(solution)/shard_map/while/body/eval_jaxpr/rhsu,ruhp->rshp/dot_general | solution.py:73
  56.3 0.0 copy-start.6
  56.3 0.0 copy-start.4
  57.0 0.2 slice_reduce_fusion.1
  57.2 0.1 multiply_bitcast_fusion
  57.3 3.4 %fusion.11 = bf16[1,512,2048]{1,2,0:T(8,128)(2,1)} fusion(f32[512,32]{0,1:T(8,128)S(1)} %multiply_bitcast_fusion, bf16[1,512,2048]{1,2,0:T(8,128)(2,1)} %bitcast.112), kind=kLoop, calls=%fused_computation.18 | loop fusion | flops 3145728 | bytes 4259840 | tf_op jit(solution)/shard_map/convert_element_type | solution.py:82
  60.7 0.0 copy-start.7
  60.7 0.0 copy-done.6
  60.7 0.1 convolution_bitcast_fusion.1
  60.9 0.0 copy-done.4
  60.9 16.3 %all_gather.7 = bf16[32,64,128]{2,1,0:T(8,128)(2,1)S(1)} all-gather(bf16[32,16,128]{2,1,0:T(8,128)(2,1)S(1)} %copy-done.4), channel_id=1, replica_groups=mesh['groups'=2,'dp'=4,'tensor'=4] {'dp'}, dimensions={1}, use_global_device_ids=true | all-gather | bytes 655360 | tf_op jit(solution)/shard_map/all_gather | solution.py:42
  77.1 0.0 all-to-all-done
  77.1 0.0 copy-start.1
  77.1 0.1 convert_bitcast_fusion
  77.2 0.1 copy.56
  77.4 0.2 add_convert_fusion
  77.6 0.0 copy-done.7
  77.6 1.1 %copy-done.1 = bf16[8,1,512,4,64]{2,4,3,1,0:T(8,128)(2,1)S(1)} copy-done((bf16[8,1,512,4,64]{2,4,3,1,0:T(8,128)(2,1)S(1)}, bf16[8,1,512,4,64]{2,4,3,1,0:T(8,128)(2,1)}, u32[]{:S(2)}) %copy-start.1) | copy-done | bytes 2097176
  78.7 5.3 %multiply_reduce_fusion = (f32[512]{0:T(512)S(1)}, f32[512,32,64]{0,2,1:T(8,128)}) fusion(f32[32]{0:T(128)S(1)} %copy-done.7, f32[512,32]{0,1:T(8,128)S(1)} %get-tuple-element.105, bf16[32,64,128]{2,1,0:T(8,128)(2,1)S(1)} %add_convert_fusion, bf16[1,512,128]{2,1,0:T(8,128)(2,1)S(1)} %copy-done.2, f32[8,1,512,4,64]{2,4,3,1,0:T(8,128)} %get-tuple-element.42, ...), kind=kOutput, calls=%fused_computation.21 | convolution fusion | flops 275774976 | bytes 11208832 | tf_op jit(solution)/shard_map/rsn,rhpn->rshp/dot_general | solution.py:86
  84.1 5.4 %copy.60 = f32[1,512,2048]{2,1,0:T(8,128)} copy(f32[1,512,2048]{1,2,0:T(8,128)} %bitcast.114) | data formatting | bytes 8388608 | tf_op jit(solution)/shard_map/reshape | solution.py:89
  89.4 0.0 copy-start.5
  89.4 2.3 %fusion.13 = bf16[1,32,64,128]{3,2,1,0:T(8,128)(2,1)S(1)} fusion(bf16[512,32,64]{0,2,1:T(8,128)(2,1)} %bitcast.115, bf16[32,64,128]{2,1,0:T(8,128)(2,1)S(1)} %add_convert_fusion, f32[32]{0:T(128)S(1)} %exp.44, bf16[1,512,128]{2,1,0:T(8,128)(2,1)S(1)} %copy-done.3), kind=kOutput, calls=%fused_computation.25 | convolution fusion | flops 269484032 | bytes 3276928 | tf_op jit(solution)/shard_map/ruhp,run->rhpn/dot_general | solution.py:83
  91.7 1.1 %copy.61 = bf16[1,32,64,128]{3,1,0,2:T(8,128)(2,1)} copy(bf16[1,32,64,128]{3,2,1,0:T(8,128)(2,1)S(1)} %fusion.13) | data formatting | bytes 1048576 | tf_op jit(solution)/shard_map/convert_element_type | solution.py:98
  92.9 3.9 %all-to-all-start.1 = ((bf16[1,32,64,128]{3,1,0,2:T(8,128)(2,1)}), bf16[1,32,64,128]{3,1,0,2:T(8,128)(2,1)S(1)}, u32[]{:S(2)}, u32[]{:S(2)}) async-start(bf16[1,32,64,128]{3,1,0,2:T(8,128)(2,1)} %copy.61), calls=%async_computation.1 | async-start | bytes 1048576 | tf_op jit(solution)/shard_map/all_to_all | solution.py:99
  96.7 0.0 copy-done.5
  96.7 4.1 %select_convert_fusion.6 = bf16[1,512,2048]{2,1,0:T(8,128)(2,1)} fusion(f32[1,512,2048]{2,1,0:T(8,128)} %copy.60, f32[2048]{0:T(1024)S(1)} %copy-done.5, f32[512]{0:T(512)S(1)} %add_rsqrt_fusion, pred[512]{0:T(512)(128)(4,1)S(1)} %fusion.19), kind=kLoop, calls=%fused_computation.20 | loop fusion | flops 4194304 | bytes 6302208 | tf_op jit(solution)/shard_map/convert_element_type | solution.py:95
  100.8 6.5 %all-to-all-done.1 = bf16[1,32,64,128]{3,1,0,2:T(8,128)(2,1)S(1)} async-done(((bf16[1,32,64,128]{3,1,0,2:T(8,128)(2,1)}), bf16[1,32,64,128]{3,1,0,2:T(8,128)(2,1)S(1)}, u32[]{:S(2)}, u32[]{:S(2)}) %all-to-all-start.1) | async-done | bytes 524320 | tf_op jit(solution)/shard_map/all_to_all | solution.py:99
  107.3 1.0 copy.70
  (31 shorter events, 0.3 us)
Async XLA Ops:
  0.6 12.8 %copy-start = (bf16[16,32,16,128]{3,2,1,0:T(8,128)(2,1)S(1)}, bf16[16,32,16,128]{3,2,1,0:T(8,128)(2,1)}, u32[]{:S(2)}) copy-start(bf16[16,32,16,128]{3,2,1,0:T(8,128)(2,1)} %param.24) | copy-start | bytes 6291460
  0.6 25.6 %copy-start.3 = (bf16[1,512,128]{2,1,0:T(8,128)(2,1)S(1)}, bf16[1,512,128]{2,1,0:T(8,128)(2,1)}, u32[]{:S(2)}) copy-start(bf16[1,512,128]{2,1,0:T(8,128)(2,1)} %param.17) | copy-start | bytes 393220
  0.7 25.6 %copy-start.2 = (bf16[1,512,128]{2,1,0:T(8,128)(2,1)S(1)}, bf16[1,512,128]{2,1,0:T(8,128)(2,1)}, u32[]{:S(2)}) copy-start(bf16[1,512,128]{2,1,0:T(8,128)(2,1)} %param.18) | copy-start | bytes 393220
  14.8 62.3 %all-to-all-start = ((bf16[4,32,16,128]{3,2,1,0:T(8,128)(2,1)}), bf16[4,32,16,128]{3,2,1,0:T(8,128)(2,1)S(1)}, u32[]{:S(2)}, u32[]{:S(2)}) async-start(bf16[4,32,16,128]{3,2,1,0:T(8,128)(2,1)} %gather_fusion), calls=%async_computation | async-start | bytes 1048576 | tf_op jit(solution)/shard_map/all_to_all | solution.py:39
  56.3 4.4 %copy-start.6 = (f32[16,32]{1,0:T(8,128)S(1)}, f32[16,32]{1,0:T(8,128)}, u32[]{:S(2)}) copy-start(f32[16,32]{1,0:T(8,128)} %param.25) | copy-start | bytes 6148
  56.3 4.5 %copy-start.4 = (bf16[32,16,128]{2,1,0:T(8,128)(2,1)S(1)}, bf16[32,16,128]{2,1,0:T(8,128)(2,1)}, u32[]{:S(2)}) copy-start(bf16[32,16,128]{2,1,0:T(8,128)(2,1)} %param.26) | copy-start | bytes 393220
  60.7 16.8 %copy-start.7 = (f32[32]{0:T(128)S(1)}, f32[32]{0:T(128)}, u32[]{:S(2)}) copy-start(f32[32]{0:T(128)} %param.22) | copy-start | bytes 388
  77.1 1.6 %copy-start.1 = (bf16[8,1,512,4,64]{2,4,3,1,0:T(8,128)(2,1)S(1)}, bf16[8,1,512,4,64]{2,4,3,1,0:T(8,128)(2,1)}, u32[]{:S(2)}) copy-start(bf16[8,1,512,4,64]{2,4,3,1,0:T(8,128)(2,1)} %get-tuple-element.175) | copy-start | bytes 6291460
  89.4 7.3 %copy-start.5 = (f32[2048]{0:T(1024)S(1)}, f32[2048]{0:T(1024)}, u32[]{:S(2)}) copy-start(f32[2048]{0:T(1024)} %param.23) | copy-start | bytes 24580
  92.9 14.5 %all-to-all-start.1 = ((bf16[1,32,64,128]{3,1,0,2:T(8,128)(2,1)}), bf16[1,32,64,128]{3,1,0,2:T(8,128)(2,1)S(1)}, u32[]{:S(2)}, u32[]{:S(2)}) async-start(bf16[1,32,64,128]{3,1,0,2:T(8,128)(2,1)} %copy.61), calls=%async_computation.1 | async-start | bytes 1048576 | tf_op jit(solution)/shard_map/all_to_all | solution.py:99
where the time goes:
time: 109 us; the launch traced here: 108 us
  matrix products  37 us (34%)
  blocking collectives  26.2 us (24%)
  local copies, waits for them, and re-layouts  16.9 us (16%)
  other arithmetic  11.4 us (10%)
  starting transfers between devices  7.33 us (7%)
  waiting for transfers between devices  6.55 us (6%)
  between operations  2.97 us (3%)
    dot_general x8, matrix products, intra_block(): jnp.einsum('rhsu,ruhp->rshp', weights, value_part, preferred_element_type...  28 us
    all_gather x1, blocking collectives, local(): whole_template = lax.all_gather(template_state, 'dp', axis=1, tiled=True)  16.3 us
    unnamed x1, blocking collectives  9.92 us
    unnamed x20, local copies, waits for them, and re-layouts  7.1 us
    all_to_all x1, waiting for transfers between devices, local(): lax.all_to_all(final_state, 'dp', split_axis=2, concat_axis=0, tiled=True)  6.55 us
    reshape x1, local copies, waits for them, and re-layouts, local(): scan.reshape(rows_here, length, heads_here // GROUP_HEADS, GROUP_HEADS *...  5.37 us
    dot_general x1, matrix products, local(): jnp.einsum('rsn,rhpn->rshp', output_proj, resumed, preferred_element_type...  5.33 us
    convert_element_type x1, other arithmetic, local(): mixed = jnp.where(keep_mask[:, :, None], normed, 0.0).astype(jnp.bfloat16)  4.06 us
  transfers between devices with their start and end apart: 2, of which 1 were waited for; matrix products, arithmetic and copies ran while one was open for 42% of the time, Pallas kernels for 0%

commit v1 on v0

v1 whole, which is shorter than its diff:
```python
import functools

import jax
import jax.numpy as jnp
from jax import lax
from jax.experimental import pallas as pl
from jax.experimental.pallas import tpu as pltpu
from jax.sharding import PartitionSpec as P

HEAD_SIZE = 64
GROUP_HEADS = 32
CHUNK = 128
LANES = 256
F32 = jnp.float32
BF16 = jnp.bfloat16
VMEM = pl.BlockSpec(memory_space=pltpu.VMEM)
SMEM = pl.BlockSpec(memory_space=pltpu.SMEM)


def split3(v):
    hi = v.astype(BF16).astype(F32)
    mid = (v - hi).astype(BF16).astype(F32)
    return hi, mid, v - hi - mid


def column(row, heads):
    eye = lax.broadcasted_iota(jnp.int32, (heads, heads), 0) == lax.broadcasted_iota(
        jnp.int32, (heads, heads), 1
    )
    return jnp.sum(jnp.where(eye, row, 0.0), axis=1, keepdims=True)


def spread_matrix(heads, lanes):
    term = lax.broadcasted_iota(jnp.int32, (128, lanes), 0)
    lane = lax.broadcasted_iota(jnp.int32, (128, lanes), 1)
    hit = ((term % heads) == (lane // HEAD_SIZE)) & (term < 3 * heads)
    return jnp.where(hit, 1.0, 0.0).astype(BF16)


def stacked(v):
    heads, length = v.shape
    hi, mid, lo = split3(v)
    full = jnp.concatenate([hi, mid, lo, jnp.zeros((128 - 3 * heads, length), F32)], axis=0)
    return full.T.astype(BF16)


def scan_steps(raw_ref, bias_ref, decay_ref, alive_count):
    heads, length = raw_ref.shape
    bias = column(bias_ref[...], heads)
    rate = -jnp.exp(column(decay_ref[...], heads))
    position = lax.broadcasted_iota(jnp.int32, (heads, length), 1)
    raw = raw_ref[...] + bias
    soft = jnp.maximum(raw, 0.0) + jnp.log1p(jnp.exp(-jnp.abs(raw)))
    step = jnp.where(position < alive_count, soft, 0.0)
    drop = rate * step
    upper = (
        lax.broadcasted_iota(jnp.int32, (CHUNK, CHUNK), 0)
        <= lax.broadcasted_iota(jnp.int32, (CHUNK, CHUNK), 1)
    )
    upper = jnp.where(upper, 1.0, 0.0).astype(BF16)
    base = jnp.zeros((heads, 1), F32)
    parts, starts = [], []
    for c in range(length // CHUNK):
        terms = jnp.concatenate(split3(drop[:, c * CHUNK : (c + 1) * CHUNK]), axis=0)
        sums = jnp.dot(terms.astype(BF16), upper, preferred_element_type=F32)
        run = sums[:heads] + sums[heads : 2 * heads] + sums[2 * heads :]
        starts.append(base)
        parts.append(run + base)
        base = base + run[:, CHUNK - 1 :]
    return step, parts, starts, base


def state_kernel(
    slot_ref, length_ref, raw_ref, bias_ref, decay_ref, x_ref, b_ref, *refs, ways, dp_name
):
    pieces, meta_ref, spread_ref, tail_ref, bt_ref, hold = (
        refs[:ways],
        refs[ways],
        refs[ways + 1],
        refs[ways + 2],
        refs[ways + 3],
        refs[ways + 4],
    )
    heads, length = raw_ref.shape
    width = heads * HEAD_SIZE
    chan = HEAD_SIZE // ways
    step, parts, _, end = scan_steps(raw_ref, bias_ref, decay_ref, length_ref[0])
    logdecay = jnp.concatenate(parts, axis=1)
    tail_ref[...] = stacked(jnp.exp(end - logdecay) * step)
    bt_ref[...] = b_ref[...].T
    spread_ref[...] = spread_matrix(heads, width)
    lane = lax.broadcasted_iota(jnp.int32, (8, 128), 1)
    eye = lax.broadcasted_iota(jnp.int32, (heads, 128), 0) == lax.broadcasted_iota(
        jnp.int32, (heads, 128), 1
    )
    last = jnp.sum(jnp.where(eye, jnp.exp(end), 0.0), axis=0, keepdims=True)
    slot = slot_ref[0].astype(F32)
    meta_ref[...] = jnp.where(lane == heads, slot, jnp.broadcast_to(last, (8, 128)))

    per = LANES // HEAD_SIZE

    def tile(t, carry):
        at = pl.ds(pl.multiple_of(t * LANES, LANES), LANES)
        scale = jnp.dot(tail_ref[...], spread_ref[:, at], preferred_element_type=F32)
        moved = (scale * x_ref[:, at].astype(F32)).astype(BF16)
        state = jnp.dot(bt_ref[...], moved, preferred_element_type=F32)
        turned = state.T.astype(BF16).reshape(per, ways, chan, 128)
        rows = pl.ds(pl.multiple_of(t * per * chan, per * chan), per * chan)
        for d in range(ways):
            hold[d, rows, :] = turned[:, d].reshape(per * chan, 128)
        return carry

    lax.fori_loop(0, width // LANES, tile, 0)
    if ways == 1:
        pieces[0][...] = hold[0]
    else:
        me = lax.axis_index(dp_name)
        for k in range(ways):
            pieces[k][...] = hold[me ^ k]


def row_spread(row, heads, rows):
    terms = jnp.concatenate(split3(row) + (jnp.zeros((1, 128 - 3 * heads), F32),), axis=1)
    lanes = jnp.broadcast_to(terms, (128, 128)).astype(BF16)
    at = lax.broadcasted_iota(jnp.int32, (rows, 128), 0) // (rows // heads)
    term = lax.broadcasted_iota(jnp.int32, (rows, 128), 1)
    pick = jnp.where((term % heads == at) & (term < 3 * heads), 1.0, 0.0).astype(BF16)
    return lax.dot_general(pick, lanes, (((1,), (1,)), ((), ())), preferred_element_type=F32)


def resume_kernel(*refs, ways, heads):
    metas, cache_ref, decay_ref, template_ref = refs[:ways], *refs[ways : ways + 3]
    outs = refs[ways + 3 :]
    rows = template_ref.shape[0]
    lane = lax.broadcasted_iota(jnp.int32, (8, 128), 1)
    template = template_ref[...].astype(F32)
    for k in range(ways):
        slot = jnp.max(jnp.where(lane == heads, metas[k][...], 0.0)).astype(jnp.int32)
        factor = row_spread(decay_ref[pl.ds(slot, 1), :], heads, rows)
        outs[k][...] = (cache_ref[slot].astype(F32) + factor * template).astype(BF16)


def intra_kernel(
    after_ref,
    length_ref,
    raw_ref,
    bias_ref,
    decay_ref,
    skip_ref,
    x_ref,
    b_ref,
    c_ref,
    y_ref,
    grow_ref,
    spread_ref,
    in_ref,
    out_ref,
    whole_ref,
    mix_ref,
    ends_ref,
):
    heads, length = raw_ref.shape
    width = heads * HEAD_SIZE
    chunks = length // CHUNK
    step, parts, starts, end = scan_steps(raw_ref, bias_ref, decay_ref, length_ref[0])
    spread_ref[...] = spread_matrix(heads, width)
    causal = lax.broadcasted_iota(jnp.int32, (CHUNK, CHUNK), 0) >= lax.broadcasted_iota(
        jnp.int32, (CHUNK, CHUNK), 1
    )
    ends = []
    for c in range(chunks):
        at = slice(c * CHUNK, (c + 1) * CHUNK)
        inside = parts[c] - starts[c]
        in_ref[at, :] = stacked(jnp.exp(-inside) * step[:, at])
        out_ref[at, :] = stacked(jnp.exp(inside))
        whole_ref[at, :] = stacked(jnp.exp(parts[c]))
        nxt = starts[c + 1] if c + 1 < chunks else end
        ends.append(jnp.exp(nxt - starts[c]))
        gram = lax.dot_general(
            c_ref[at, :], b_ref[at, :], (((1,), (1,)), ((), ())), preferred_element_type=F32
        )
        mix_ref[at, :CHUNK] = jnp.where(causal, gram, 0.0).astype(BF16)
        mix_ref[at, CHUNK:] = c_ref[at, :]
    lane = lax.broadcasted_iota(jnp.int32, (heads, 128), 1)
    pad = jnp.zeros((heads, 128), F32)
    for c in range(chunks):
        pad = jnp.where(lane == c, ends[c], pad)
    ends_ref[...] = stacked(pad)
    skip_row = jnp.concatenate(split3(skip_ref[...]) + (jnp.zeros((1, 128 - 3 * heads), F32),), axis=1)
    skip_rows = jnp.broadcast_to(skip_row, (8, 128)).astype(BF16)

    def tile(t, carry):
        at = pl.ds(pl.multiple_of(t * LANES, LANES), LANES)
        hot = spread_ref[:, at]
        skip = jnp.dot(skip_rows, hot, preferred_element_type=F32)[0:1]
        decay = jnp.dot(ends_ref[0:8, :], hot, preferred_element_type=F32)
        state = jnp.zeros((128, LANES), F32)
        for c in range(chunks):
            rows = slice(c * CHUNK, (c + 1) * CHUNK)
            x = x_ref[rows, at].astype(F32)
            inner = jnp.dot(in_ref[rows, :], hot, preferred_element_type=F32)
            moved = (x * inner).astype(BF16)
            both = jnp.concatenate([moved, state.astype(BF16)], axis=0)
            mixed = jnp.dot(mix_ref[rows, :], both, preferred_element_type=F32)
            outer = jnp.dot(out_ref[rows, :], hot, preferred_element_type=F32)
            y_ref[rows, at] = outer * mixed + skip * x
            grow_ref[rows, at] = jnp.dot(whole_ref[rows, :], hot, preferred_element_type=F32)
            if c + 1 < chunks:
                fresh = lax.dot_general(
                    b_ref[rows, :], moved, (((0,), (0,)), ((), ())), preferred_element_type=F32
                )
                state = decay[c : c + 1] * (state + fresh)
        return carry

    lax.fori_loop(0, width // LANES, tile, 0)


def norm_kernel(length_ref, offset_ref, *refs, ways, dp_name, heads, block):
    pieces = refs[:ways]
    y_ref, grow_ref, c_ref, gain_ref, mixed_ref, hold = refs[ways:]
    chan = HEAD_SIZE // ways
    i = pl.program_id(0)

    @pl.when(i == 0)
    def _():
        if ways == 1:
            hold[...] = pieces[0][...]
        else:
            me = lax.axis_index(dp_name)
            for k in range(ways):
                start = pl.multiple_of((me ^ k) * chan, chan)
                for h in range(heads):
                    hold[pl.ds(h * HEAD_SIZE + start, chan), :] = pieces[k][
                        h * chan : (h + 1) * chan, :
                    ]

    rows = pl.ds(pl.multiple_of(i * block, block), block)
    carried = lax.dot_general(
        c_ref[rows, :], hold[...], (((1,), (1,)), ((), ())), preferred_element_type=F32
    )
    scan = y_ref[rows, :] + grow_ref[rows, :] * carried
    meansq = jnp.mean(scan * scan, axis=1, keepdims=True)
    position = lax.broadcasted_iota(jnp.int32, (block, 1), 0) + i * block
    keep = (position < length_ref[0]) & (position >= offset_ref[0])
    factor = jnp.where(keep, lax.rsqrt(meansq + 1e-05), 0.0)
    mixed_ref[0] = (scan * factor * gain_ref[...]).astype(BF16)


def final_kernel(*refs, ways, dp_name, heads):
    pieces, resumed, metas = refs[:ways], refs[ways : 2 * ways], refs[2 * ways : 3 * ways]
    out_ref = refs[3 * ways]
    rows = pieces[0].shape[0]
    me = lax.axis_index(dp_name)
    for k in range(ways):
        whole = row_spread(metas[k][0:1, :heads], heads, rows)
        out_ref[me ^ k] = (
            pieces[k][...].astype(F32) + whole * resumed[k][...].astype(F32)
        ).astype(BF16)


def cost(flops, size):
    return pl.CostEstimate(flops=flops, bytes_accessed=size, transcendentals=0)


def local(
    ssm_input,
    input_proj,
    output_proj,
    step_raw,
    step_bias,
    decay_log,
    skip_gain,
    norm_gain,
    cache_states,
    slot_decay,
    template_state,
    slot_ids,
    row_lengths,
    row_offsets,
    *,
    dp,
):
    _, length, width = ssm_input.shape
    heads = step_raw.shape[1]
    slots, _, chan, state = cache_states.shape
    direct = dp in (2, 4)
    ways = dp if direct else 1
    rows = heads * HEAD_SIZE // ways
    x, b, c, raw = ssm_input[0], input_proj[0], output_proj[0], step_raw[0]
    bias, decay, skip = step_bias[None], decay_log[None], skip_gain[None]
    piece = jax.ShapeDtypeStruct((rows, state), BF16)
    params = pltpu.CompilerParams(vmem_limit_bytes=24 << 20)

    *local_parts, meta = pl.pallas_call(
        functools.partial(state_kernel, ways=ways, dp_name="dp"),
        out_shape=[piece] * ways + [jax.ShapeDtypeStruct((8, 128), F32)],
        in_specs=[SMEM, SMEM] + [VMEM] * 5,
        out_specs=[VMEM] * (ways + 1),
        scratch_shapes=[
            pltpu.VMEM((128, width), BF16),
            pltpu.VMEM((length, 128), BF16),
            pltpu.VMEM((128, length), BF16),
            pltpu.VMEM((ways, rows, state), BF16),
        ],
        compiler_params=params,
        cost_estimate=cost(2 * length * width * 256, 3 << 20),
        name="state",
    )(slot_ids, row_lengths, raw, bias, decay, x, b)

    def intra(after):
        return pl.pallas_call(
            intra_kernel,
            out_shape=[jax.ShapeDtypeStruct((length, width), F32)] * 2,
            in_specs=[VMEM, SMEM] + [VMEM] * 7,
            out_specs=[VMEM] * 2,
            scratch_shapes=[
                pltpu.VMEM((128, width), BF16),
                pltpu.VMEM((length, 128), BF16),
                pltpu.VMEM((length, 128), BF16),
                pltpu.VMEM((length, 128), BF16),
                pltpu.VMEM((length, 2 * CHUNK), BF16),
                pltpu.VMEM((128, 128), BF16),
            ],
            compiler_params=params,
            cost_estimate=cost(2 * length * width * 1024, 16 << 20),
            name="intra",
        )(after, row_lengths, raw, bias, decay, skip, x, b, c)

    if direct:

        def swap(v, k):
            return lax.ppermute(v, "dp", [(i, i ^ k) for i in range(dp)])

        order = [2, 3, 1] if dp == 4 else [1]
        got = {k: swap(local_parts[k], k) for k in order}
        metas = {0: meta, **{k: swap(meta, k) for k in order}}
        metas = [metas[k] for k in range(dp)]
        resumed = pl.pallas_call(
            functools.partial(resume_kernel, ways=dp, heads=heads),
            out_shape=[piece] * dp,
            in_specs=[VMEM] * (dp + 3),
            out_specs=[VMEM] * dp,
            compiler_params=params,
            cost_estimate=cost(2 * rows * 128 * 128 * dp, 2 << 20),
            name="resume",
        )(
            *metas,
            cache_states.reshape(slots, rows, state),
            slot_decay,
            template_state.reshape(rows, state),
        )
        sent = {k: swap(resumed[k], k) for k in order}
        y, grow = intra(resumed[0][:8, :])
        final = pl.pallas_call(
            functools.partial(final_kernel, ways=dp, dp_name="dp", heads=heads),
            out_shape=jax.ShapeDtypeStruct((dp, rows, state), BF16),
            in_specs=[VMEM] * (3 * dp),
            out_specs=VMEM,
            compiler_params=params,
            cost_estimate=cost(2 * rows * 128 * 128 * dp, 2 << 20),
            name="final",
        )(local_parts[0], *[got[k] for k in range(1, dp)], *resumed, *metas)
        new_states = final.reshape(dp, heads, chan, state)
        arrived = [resumed[0]] + [sent[k] for k in range(1, dp)]
    else:
        metas = lax.all_gather(meta[0], "dp", axis=0)
        ids = metas[:, heads].astype(jnp.int32)
        resumed = (
            cache_states[ids].astype(F32)
            + slot_decay[ids][:, :, None, None] * template_state.astype(F32)[None]
        ).astype(BF16)
        mine = lax.all_to_all(resumed, "dp", split_axis=0, concat_axis=2, tiled=True)
        arrived = [mine.reshape(rows, state)]
        given = lax.all_to_all(
            local_parts[0].reshape(1, heads, HEAD_SIZE, state),
            "dp",
            split_axis=2,
            concat_axis=0,
            tiled=True,
        )
        new_states = (
            given.astype(F32) + metas[:, :heads, None, None] * resumed.astype(F32)
        ).astype(BF16)
        y, grow = intra(local_parts[0][:8, :])

    block = CHUNK
    mixed = pl.pallas_call(
        functools.partial(norm_kernel, ways=ways, dp_name="dp", heads=heads, block=block),
        out_shape=jax.ShapeDtypeStruct((1, length, width), BF16),
        grid=(length // block,),
        in_specs=[SMEM, SMEM] + [VMEM] * (ways + 4),
        out_specs=pl.BlockSpec((1, block, width), lambda i: (0, i, 0)),
        scratch_shapes=[pltpu.VMEM((heads * HEAD_SIZE, state), BF16)],
        compiler_params=params,
        cost_estimate=cost(2 * length * width * 128, 4 << 20),
        name="norm",
    )(row_lengths, row_offsets, *arrived, y, grow, c, norm_gain[None])
    return (mixed, new_states)


def solution(mesh):
    return jax.shard_map(
        functools.partial(local, dp=mesh.shape["dp"]),
        mesh=mesh,
        in_specs=(
            P(("groups", "dp"), None, "tensor"),
            P(("groups", "dp"), None, "tensor"),
            P(("groups", "dp"), None, "tensor"),
            P(("groups", "dp"), "tensor", None),
            P("tensor"),
            P("tensor"),
            P("tensor"),
            P("tensor"),
            P("groups", "tensor", "dp", None),
            P("groups", "tensor"),
            P(("groups", "tensor"), "dp", None),
            P(("groups", "dp")),
            P(("groups", "dp")),
            P(("groups", "dp")),
        ),
        out_specs=(P(("groups", "dp"), None, "tensor"), P("groups", "tensor", "dp", None)),
        check_vma=False,
    )
```

time: 109 us -> 44.6 us (0.41)
  matrix products: 37 us -> 0 us
  blocking collectives: 26.2 us -> 0 us
  Pallas kernels: 0 us -> 18.6 us
  other arithmetic: 11.4 us -> 0 us
  local copies, waits for them, and re-layouts: 16.9 us -> 6.27 us
  starting transfers between devices: 7.33 us -> 14.8 us
  waiting for transfers between devices: 6.55 us -> 1.77 us
    dot_general x12 -> x0, matrix products: 37 us -> none  [the longest x8 28 us: intra_block(): jnp.einsum('rhsu,ruhp->rshp', weights, value_part, preferred_element_type...]
    pallas_call x0 -> x5, Pallas kernels: none -> 18.6 us  [the longest x1 9.3 us: intra(): pl.pallas_call(intra_kernel, out_shape=[jax.ShapeDtypeStruct((length, wid...]
    all_gather x1 -> x0, blocking collectives: 16.3 us -> none  [local(): whole_template = lax.all_gather(template_state, 'dp', axis=1, tiled=True)]
    ppermute x0 -> x9, starting transfers between devices: none -> 14.8 us  [swap(): return lax.ppermute(v, 'dp', [(i, i ^ k) for i in range(dp)])]
    unnamed x1 -> x0, blocking collectives: 9.92 us -> none
    convert_element_type x4 -> x0, other arithmetic: 7.75 us -> none  [the longest x1 4.06 us: local(): mixed = jnp.where(keep_mask[:, :, None], normed, 0.0).astype(jnp.bfloat16)]
    all_to_all x2 -> x0, starting transfers between devices: 7.33 us -> none  [the longest x1 3.85 us: local(): lax.all_to_all(final_state, 'dp', split_axis=2, concat_axis=0, tiled=True)]
    all_to_all x2 -> x0, waiting for transfers between devices: 6.55 us -> none  [the longest x1 6.55 us: local(): lax.all_to_all(final_state, 'dp', split_axis=2, concat_axis=0, tiled=True)]
  transfers between devices with their start and end apart: 2 -> 9, of which waited for: 1 -> 2; matrix products, arithmetic and copies ran while one was open for 42% -> 0% of each run, Pallas kernels for 0% -> 25%
where the time goes in v1:
time: 44.6 us; the launch traced here: 44.3 us
  Pallas kernels  18.6 us (42%)
  starting transfers between devices  14.8 us (33%)
  local copies, waits for them, and re-layouts  6.27 us (14%)
  between operations  2.83 us (6%)
  waiting for transfers between devices  1.77 us (4%)
    ppermute x9, starting transfers between devices, swap(): return lax.ppermute(v, 'dp', [(i, i ^ k) for i in range(dp)])  14.8 us
    pallas_call x1, Pallas kernels, intra(): pl.pallas_call(intra_kernel, out_shape=[jax.ShapeDtypeStruct((length, wid...  9.3 us
    unnamed x28, local copies, waits for them, and re-layouts  6.26 us
    pallas_call x1, Pallas kernels, local(): pl.pallas_call(functools.partial(state_kernel, ways=ways, dp_name='dp'),...  4.43 us
    pallas_call x1, Pallas kernels, local(): pl.pallas_call(functools.partial(norm_kernel, ways=ways, dp_name='dp', he...  3.17 us
    ppermute x9, waiting for transfers between devices, swap(): return lax.ppermute(v, 'dp', [(i, i ^ k) for i in range(dp)])  1.77 us
    pallas_call x1, Pallas kernels, local(): pl.pallas_call(functools.partial(final_kernel, ways=dp, dp_name='dp', hea...  1.22 us
  transfers between devices with their start and end apart: 9, of which 2 were waited for; matrix products, arithmetic and copies ran while one was open for 0% of the time, Pallas kernels for 25%

profile of v1, /device:TPU:0, one launch (start us, length us, event | category | flops | bytes accessed | tf_op | source)
XLA Modules:
  0.0 44.3 jit_solution(3953910643699639151)
XLA Ops:
  0.6 0.0 copy-start
  2.1 0.0 copy-start.1
  2.1 1.6 %copy-done.1 = bf16[1,512,2048]{2,1,0:T(8,128)(2,1)S(1)} copy-done((bf16[1,512,2048]{2,1,0:T(8,128)(2,1)S(1)}, bf16[1,512,2048]{2,1,0:T(8,128)(2,1)}, u32[]{:S(2)}) %copy-start.1) | copy-done | bytes 2097176
  3.7 0.0 copy-start.5
  3.7 0.9 %copy-done.5 = bf16[1,512,128]{2,1,0:T(8,128)(2,1)S(1)} copy-done((bf16[1,512,128]{2,1,0:T(8,128)(2,1)S(1)}, bf16[1,512,128]{2,1,0:T(8,128)(2,1)}, u32[]{:S(2)}) %copy-start.5) | copy-done | bytes 131096
  4.6 0.0 copy-start.7
  4.6 0.8 %copy-done.7 = f32[1,32,512]{2,1,0:T(8,128)S(1)} copy-done((f32[1,32,512]{2,1,0:T(8,128)S(1)}, f32[1,32,512]{2,1,0:T(8,128)}, u32[]{:S(2)}) %copy-start.7) | copy-done | bytes 65560
  5.4 0.0 copy-start.11
  5.4 0.7 %copy-done.11 = f32[32]{0:T(128)S(1)} copy-done((f32[32]{0:T(128)S(1)}, f32[32]{0:T(128)}, u32[]{:S(2)}) %copy-start.11) | copy-done | bytes 152
  6.1 0.0 copy-start.12
  6.1 0.7 %copy-done.12 = f32[32]{0:T(128)S(1)} copy-done((f32[32]{0:T(128)S(1)}, f32[32]{0:T(128)}, u32[]{:S(2)}) %copy-start.12) | copy-done | bytes 152
  6.7 0.0 copy-start.2
  6.7 0.0 copy-start.3
  6.7 4.4 %state.1 = (bf16[512,128]{1,0:T(8,128)(2,1)S(1)}, bf16[512,128]{1,0:T(8,128)(2,1)S(1)}, bf16[512,128]{1,0:T(8,128)(2,1)S(1)}, bf16[512,128]{1,0:T(8,128)(2,1)S(1)}, f32[8,128]{1,0:T(8,128)S(1)}) custom-call(s32[1]{0:T(128)S(6)} %copy.16.slot_ref, s32[1]{0:T(128)S(6)} %copy.17.length_ref, f32[32,512]{1,0:T(8,128)S(1)} %bitcast.19, f32[1,32]{1,0:T(1,128)S(1)} %bitcast.22, ...), custom_call_target="tpu_custom_call" | custom-call | flops 536870912 | bytes 3145728 | tf_op jit(solution)/shard_map/state/pallas_call | solution.py:294
  11.2 3.1 %collective-permute-start.6 = (bf16[512,128]{1,0:T(8,128)(2,1)S(1)}, bf16[512,128]{1,0:T(8,128)(2,1)S(1)}, u32[]{:S(2)}, u32[]{:S(2)}) collective-permute-start(bf16[512,128]{1,0:T(8,128)(2,1)S(1)} %get-tuple-element.21), channel_id=1, source_target_pairs={{0,4},{4,0},{8,12},{12,8},{1,5},{5,1},{9,13},{13,9},{2,6},{6,2},{1... | collective-permute-start | bytes 393224 | tf_op jit(solution)/shard_map/ppermute | solution.py:332
  14.3 2.5 %collective-permute-start.2 = (f32[8,128]{1,0:T(8,128)S(1)}, f32[8,128]{1,0:T(8,128)S(1)}, u32[]{:S(2)}, u32[]{:S(2)}) collective-permute-start(f32[8,128]{1,0:T(8,128)S(1)} %get-tuple-element.13.refs_0_.refs_8_), channel_id=1, source_target_pairs={{0,12},{4,8},{8,4},{12,0},{1,13},{5,9},{9,5},{13,1},{2,14},{6,10},... | collective-permute-start | bytes 12296 | tf_op jit(solution)/shard_map/ppermute | solution.py:332
  16.8 0.1 collective-permute-start.1
  16.9 1.8 %collective-permute-start = (f32[8,128]{1,0:T(8,128)S(1)}, f32[8,128]{1,0:T(8,128)S(1)}, u32[]{:S(2)}, u32[]{:S(2)}) collective-permute-start(f32[8,128]{1,0:T(8,128)S(1)} %get-tuple-element.13.refs_0_.refs_8_), channel_id=1, source_target_pairs={{0,4},{4,0},{8,12},{12,8},{1,5},{5,1},{9,13},{13,9},{2,6},{6,2},{1... | collective-permute-start | bytes 12296 | tf_op jit(solution)/shard_map/ppermute | solution.py:332
  18.7 1.7 %collective-permute-start.7 = (bf16[512,128]{1,0:T(8,128)(2,1)S(1)}, bf16[512,128]{1,0:T(8,128)(2,1)S(1)}, u32[]{:S(2)}, u32[]{:S(2)}) collective-permute-start(bf16[512,128]{1,0:T(8,128)(2,1)S(1)} %get-tuple-element.22), channel_id=1, source_target_pairs={{0,8},{4,12},{8,0},{12,4},{1,9},{5,13},{9,1},{13,5},{2,10},{6,14},... | collective-permute-start | bytes 393224 | tf_op jit(solution)/shard_map/ppermute | solution.py:332
  21.0 0.0 collective-permute-done.2.refs_3_.refs_11_
  21.0 1.1 %collective-permute-start.8 = (bf16[512,128]{1,0:T(8,128)(2,1)S(1)}, bf16[512,128]{1,0:T(8,128)(2,1)S(1)}, u32[]{:S(2)}, u32[]{:S(2)}) collective-permute-start(bf16[512,128]{1,0:T(8,128)(2,1)S(1)} %get-tuple-element.23), channel_id=1, source_target_pairs={{0,12},{4,8},{8,4},{12,0},{1,13},{5,9},{9,5},{13,1},{2,14},{6,10},... | collective-permute-start | bytes 393224 | tf_op jit(solution)/shard_map/ppermute | solution.py:332
  22.2 0.2 collective-permute-done.1.refs_2_.refs_10_
  22.4 0.0 collective-permute-done.refs_1_.refs_9_
  22.4 0.0 copy-done
  22.4 0.0 copy-start.4
  22.4 0.9 %copy-done.4 = bf16[32,16,128]{2,1,0:T(8,128)(2,1)S(1)} copy-done((bf16[32,16,128]{2,1,0:T(8,128)(2,1)S(1)}, bf16[32,16,128]{2,1,0:T(8,128)(2,1)}, u32[]{:S(2)}) %copy-start.4) | copy-done | bytes 131096
  23.3 0.0 copy-start.9
  23.3 0.7 %copy-done.9 = f32[16,32]{1,0:T(8,128)S(1)} copy-done((f32[16,32]{1,0:T(8,128)S(1)}, f32[16,32]{1,0:T(8,128)}, u32[]{:S(2)}) %copy-start.9) | copy-done | bytes 2072
  24.0 0.0 copy-start.6
  24.0 0.0 copy-start.8
  24.0 0.0 copy-start.13
  24.0 0.5 %resume.1 = (bf16[512,128]{1,0:T(8,128)(2,1)S(1)}, bf16[512,128]{1,0:T(8,128)(2,1)S(1)}, bf16[512,128]{1,0:T(8,128)(2,1)S(1)}, bf16[512,128]{1,0:T(8,128)(2,1)S(1)}) custom-call(f32[8,128]{1,0:T(8,128)S(1)} %get-tuple-element.13.refs_0_.refs_8_, f32[8,128]{1,0:T(8,128)S(1)} %collective-permute-done.refs_1_.refs_9_, ...), custom_call_target="tpu_custom_call" | custom-call | flops 67108864 | bytes 2097152 | tf_op jit(solution)/shard_map/resume/pallas_call | solution.py:338
  24.5 0.6 %collective-permute-start.3 = (bf16[512,128]{1,0:T(8,128)(2,1)S(1)}, bf16[512,128]{1,0:T(8,128)(2,1)S(1)}, u32[]{:S(2)}, u32[]{:S(2)}) collective-permute-start(bf16[512,128]{1,0:T(8,128)(2,1)S(1)} %get-tuple-element.15.refs_5_), channel_id=1, source_target_pairs={{0,4},{4,0},{8,12},{12,8},{1,5},{5,1},{9,13},{13,9},{2,6},{6,2},{1... | collective-permute-start | bytes 393224 | tf_op jit(solution)/shard_map/ppermute | solution.py:332
  25.1 2.6 %collective-permute-start.4 = (bf16[512,128]{1,0:T(8,128)(2,1)S(1)}, bf16[512,128]{1,0:T(8,128)(2,1)S(1)}, u32[]{:S(2)}, u32[]{:S(2)}) collective-permute-start(bf16[512,128]{1,0:T(8,128)(2,1)S(1)} %get-tuple-element.16.refs_6_), channel_id=1, source_target_pairs={{0,8},{4,12},{8,0},{12,4},{1,9},{5,13},{9,1},{13,5},{2,10},{6,14},... | collective-permute-start | bytes 393224 | tf_op jit(solution)/shard_map/ppermute | solution.py:332
  27.7 0.0 collective-permute-done.6.refs_1_
  27.7 1.3 %collective-permute-start.5 = (bf16[512,128]{1,0:T(8,128)(2,1)S(1)}, bf16[512,128]{1,0:T(8,128)(2,1)S(1)}, u32[]{:S(2)}, u32[]{:S(2)}) collective-permute-start(bf16[512,128]{1,0:T(8,128)(2,1)S(1)} %get-tuple-element.17.refs_7_), channel_id=1, source_target_pairs={{0,12},{4,8},{8,4},{12,0},{1,13},{5,9},{9,5},{13,1},{2,14},{6,10},... | collective-permute-start | bytes 393224 | tf_op jit(solution)/shard_map/ppermute | solution.py:332
  29.0 0.0 copy-done.2
  29.0 0.0 copy-done.3
  29.0 0.0 copy-done.6
  29.0 0.0 copy-done.8
  29.0 0.0 copy-done.13
  29.0 0.0 copy-start.10
  29.0 9.3 %intra.1 = (f32[512,2048]{1,0:T(8,128)S(1)}, f32[512,2048]{1,0:T(8,128)S(1)}) custom-call(bf16[8,128]{1,0:T(8,128)(2,1)S(1)} %slice.3.after_ref, s32[1]{0:T(128)S(6)} %copy.17.length_ref, f32[32,512]{1,0:T(8,128)S(1)} %bitcast.20, f32[1,32]{1,0:T(1,128)S(1)} %bitcast.23, f32[1,32]{1,0:T(1,128)S(1)} %bitcast.25, f32[1,32]{1,0:T(1,128)S(1)} %bitcast.26, ...), custom_call_target="tpu_custom_call" | custom-call | flops 2147483648 | bytes 16777216 | tf_op jit(solution)/shard_map/intra/pallas_call | solution.py:311
  38.3 0.0 collective-permute-done.7.refs_2_
  38.3 0.0 collective-permute-done.8.refs_3_
  38.3 1.2 %final.1 = bf16[4,512,128]{2,1,0:T(8,128)(2,1)} custom-call(bf16[512,128]{1,0:T(8,128)(2,1)S(1)} %get-tuple-element.20.refs_0_, bf16[512,128]{1,0:T(8,128)(2,1)S(1)} %collective-permute-done.6.refs_1_, bf16[512,128]{1,0:T(8,128)(2,1)S(1)} %collective-permute-done.7.refs_2_, bf16[512,128]{1,0:T(8,128)(2,1)S(1)} %collective-permute-done.8.refs_3_, ...), custom_call_target="tpu_custom_call" | custom-call | flops 67108864 | bytes 2097152 | tf_op jit(solution)/shard_map/final/pallas_call | solution.py:354
  39.6 0.0 collective-permute-done.3.refs_1_
  39.6 1.5 %collective-permute-done.4.refs_2_ = bf16[512,128]{1,0:T(8,128)(2,1)S(1)} collective-permute-done((bf16[512,128]{1,0:T(8,128)(2,1)S(1)}, bf16[512,128]{1,0:T(8,128)(2,1)S(1)}, u32[]{:S(2)}, u32[]{:S(2)}) %collective-permute-start.4) | collective-permute-done | bytes 131104 | tf_op jit(solution)/shard_map/ppermute | solution.py:332
  41.1 0.0 collective-permute-done.5.refs_3_
  41.1 0.0 copy-done.10
  41.1 3.2 %norm.1 = bf16[1,512,2048]{2,1,0:T(8,128)(2,1)} custom-call(s32[1]{0:T(128)S(6)} %copy.17.length_ref, s32[1]{0:T(128)S(6)} %copy.18.offset_ref, bf16[512,128]{1,0:T(8,128)(2,1)S(1)} %get-tuple-element.14.refs_0_.refs_4_, bf16[512,128]{1,0:T(8,128)(2,1)S(1)} %collective-permute-done.3.refs_1_, bf16[512,128]{1,0:T(8,128)(2,1)S(1)} %collective-permute-done.4.refs_2_, ...), custom_call_target="tpu_custom_call" | custom-call | flops 268435456 | bytes 4194304 | tf_op jit(solution)/shard_map/norm/pallas_call | solution.py:387
  (1 shorter events, 0.0 us)
Async XLA Ops:
  0.6 21.8 %copy-start = (bf16[16,32,16,128]{3,2,1,0:T(8,128)(2,1)S(1)}, bf16[16,32,16,128]{3,2,1,0:T(8,128)(2,1)}, u32[]{:S(2)}) copy-start(bf16[16,32,16,128]{3,2,1,0:T(8,128)(2,1)} %param.22) | copy-start | bytes 6291460
  2.1 1.6 %copy-start.1 = (bf16[1,512,2048]{2,1,0:T(8,128)(2,1)S(1)}, bf16[1,512,2048]{2,1,0:T(8,128)(2,1)}, u32[]{:S(2)}) copy-start(bf16[1,512,2048]{2,1,0:T(8,128)(2,1)} %param.14) | copy-start | bytes 6291460
  3.7 0.9 %copy-start.5 = (bf16[1,512,128]{2,1,0:T(8,128)(2,1)S(1)}, bf16[1,512,128]{2,1,0:T(8,128)(2,1)}, u32[]{:S(2)}) copy-start(bf16[1,512,128]{2,1,0:T(8,128)(2,1)} %param.15) | copy-start | bytes 393220
  4.6 0.8 %copy-start.7 = (f32[1,32,512]{2,1,0:T(8,128)S(1)}, f32[1,32,512]{2,1,0:T(8,128)}, u32[]{:S(2)}) copy-start(f32[1,32,512]{2,1,0:T(8,128)} %param.17) | copy-start | bytes 196612
  5.4 0.7 %copy-start.11 = (f32[32]{0:T(128)S(1)}, f32[32]{0:T(128)}, u32[]{:S(2)}) copy-start(f32[32]{0:T(128)} %param.18) | copy-start | bytes 388
  6.1 0.7 %copy-start.12 = (f32[32]{0:T(128)S(1)}, f32[32]{0:T(128)}, u32[]{:S(2)}) copy-start(f32[32]{0:T(128)} %param.19) | copy-start | bytes 388
  6.7 22.3 %copy-start.2 = (bf16[1,512,2048]{2,1,0:T(8,128)(2,1)S(1)}, bf16[1,512,2048]{2,1,0:T(8,128)(2,1)}, u32[]{:S(2)}) copy-start(bf16[1,512,2048]{2,1,0:T(8,128)(2,1)} %param.14) | copy-start | bytes 6291460
  6.7 22.3 %copy-start.3 = (bf16[1,512,128]{2,1,0:T(8,128)(2,1)S(1)}, bf16[1,512,128]{2,1,0:T(8,128)(2,1)}, u32[]{:S(2)}) copy-start(bf16[1,512,128]{2,1,0:T(8,128)(2,1)} %param.16) | copy-start | bytes 393220
  11.2 16.5 %collective-permute-start.6 = (bf16[512,128]{1,0:T(8,128)(2,1)S(1)}, bf16[512,128]{1,0:T(8,128)(2,1)S(1)}, u32[]{:S(2)}, u32[]{:S(2)}) collective-permute-start(bf16[512,128]{1,0:T(8,128)(2,1)S(1)} %get-tuple-element.21), channel_id=1, source_target_pairs={{0,4},{4,0},{8,12},{12,8},{1,5},{5,1},{9,13},{13,9},{2,6},{6,2},{1... | collective-permute-start | bytes 393224 | tf_op jit(solution)/shard_map/ppermute | solution.py:332
  14.3 6.7 %collective-permute-start.2 = (f32[8,128]{1,0:T(8,128)S(1)}, f32[8,128]{1,0:T(8,128)S(1)}, u32[]{:S(2)}, u32[]{:S(2)}) collective-permute-start(f32[8,128]{1,0:T(8,128)S(1)} %get-tuple-element.13.refs_0_.refs_8_), channel_id=1, source_target_pairs={{0,12},{4,8},{8,4},{12,0},{1,13},{5,9},{9,5},{13,1},{2,14},{6,10},... | collective-permute-start | bytes 12296 | tf_op jit(solution)/shard_map/ppermute | solution.py:332
  16.8 5.6 %collective-permute-start.1 = (f32[8,128]{1,0:T(8,128)S(1)}, f32[8,128]{1,0:T(8,128)S(1)}, u32[]{:S(2)}, u32[]{:S(2)}) collective-permute-start(f32[8,128]{1,0:T(8,128)S(1)} %get-tuple-element.13.refs_0_.refs_8_), channel_id=1, source_target_pairs={{0,8},{4,12},{8,0},{12,4},{1,9},{5,13},{9,1},{13,5},{2,10},{6,14},... | collective-permute-start | bytes 12296 | tf_op jit(solution)/shard_map/ppermute | solution.py:332
  16.9 5.5 %collective-permute-start = (f32[8,128]{1,0:T(8,128)S(1)}, f32[8,128]{1,0:T(8,128)S(1)}, u32[]{:S(2)}, u32[]{:S(2)}) collective-permute-start(f32[8,128]{1,0:T(8,128)S(1)} %get-tuple-element.13.refs_0_.refs_8_), channel_id=1, source_target_pairs={{0,4},{4,0},{8,12},{12,8},{1,5},{5,1},{9,13},{13,9},{2,6},{6,2},{1... | collective-permute-start | bytes 12296 | tf_op jit(solution)/shard_map/ppermute | solution.py:332
  18.7 19.6 %collective-permute-start.7 = (bf16[512,128]{1,0:T(8,128)(2,1)S(1)}, bf16[512,128]{1,0:T(8,128)(2,1)S(1)}, u32[]{:S(2)}, u32[]{:S(2)}) collective-permute-start(bf16[512,128]{1,0:T(8,128)(2,1)S(1)} %get-tuple-element.22), channel_id=1, source_target_pairs={{0,8},{4,12},{8,0},{12,4},{1,9},{5,13},{9,1},{13,5},{2,10},{6,14},... | collective-permute-start | bytes 393224 | tf_op jit(solution)/shard_map/ppermute | solution.py:332
  21.0 17.3 %collective-permute-start.8 = (bf16[512,128]{1,0:T(8,128)(2,1)S(1)}, bf16[512,128]{1,0:T(8,128)(2,1)S(1)}, u32[]{:S(2)}, u32[]{:S(2)}) collective-permute-start(bf16[512,128]{1,0:T(8,128)(2,1)S(1)} %get-tuple-element.23), channel_id=1, source_target_pairs={{0,12},{4,8},{8,4},{12,0},{1,13},{5,9},{9,5},{13,1},{2,14},{6,10},... | collective-permute-start | bytes 393224 | tf_op jit(solution)/shard_map/ppermute | solution.py:332
  22.4 0.9 %copy-start.4 = (bf16[32,16,128]{2,1,0:T(8,128)(2,1)S(1)}, bf16[32,16,128]{2,1,0:T(8,128)(2,1)}, u32[]{:S(2)}) copy-start(bf16[32,16,128]{2,1,0:T(8,128)(2,1)} %param.24) | copy-start | bytes 393220
  23.3 0.7 %copy-start.9 = (f32[16,32]{1,0:T(8,128)S(1)}, f32[16,32]{1,0:T(8,128)}, u32[]{:S(2)}) copy-start(f32[16,32]{1,0:T(8,128)} %refs_5_.1) | copy-start | bytes 6148
  24.0 5.0 %copy-start.6 = (bf16[1,512,128]{2,1,0:T(8,128)(2,1)S(1)}, bf16[1,512,128]{2,1,0:T(8,128)(2,1)}, u32[]{:S(2)}) copy-start(bf16[1,512,128]{2,1,0:T(8,128)(2,1)} %param.15) | copy-start | bytes 393220
  24.0 5.0 %copy-start.8 = (f32[1,32,512]{2,1,0:T(8,128)S(1)}, f32[1,32,512]{2,1,0:T(8,128)}, u32[]{:S(2)}) copy-start(f32[1,32,512]{2,1,0:T(8,128)} %param.17) | copy-start | bytes 196612
  24.0 5.0 %copy-start.13 = (f32[32]{0:T(128)S(1)}, f32[32]{0:T(128)}, u32[]{:S(2)}) copy-start(f32[32]{0:T(128)} %param.20) | copy-start | bytes 388
  24.5 15.0 %collective-permute-start.3 = (bf16[512,128]{1,0:T(8,128)(2,1)S(1)}, bf16[512,128]{1,0:T(8,128)(2,1)S(1)}, u32[]{:S(2)}, u32[]{:S(2)}) collective-permute-start(bf16[512,128]{1,0:T(8,128)(2,1)S(1)} %get-tuple-element.15.refs_5_), channel_id=1, source_target_pairs={{0,4},{4,0},{8,12},{12,8},{1,5},{5,1},{9,13},{13,9},{2,6},{6,2},{1... | collective-permute-start | bytes 393224 | tf_op jit(solution)/shard_map/ppermute | solution.py:332
  25.1 16.0 %collective-permute-start.4 = (bf16[512,128]{1,0:T(8,128)(2,1)S(1)}, bf16[512,128]{1,0:T(8,128)(2,1)S(1)}, u32[]{:S(2)}, u32[]{:S(2)}) collective-permute-start(bf16[512,128]{1,0:T(8,128)(2,1)S(1)} %get-tuple-element.16.refs_6_), channel_id=1, source_target_pairs={{0,8},{4,12},{8,0},{12,4},{1,9},{5,13},{9,1},{13,5},{2,10},{6,14},... | collective-permute-start | bytes 393224 | tf_op jit(solution)/shard_map/ppermute | solution.py:332
  27.7 13.4 %collective-permute-start.5 = (bf16[512,128]{1,0:T(8,128)(2,1)S(1)}, bf16[512,128]{1,0:T(8,128)(2,1)S(1)}, u32[]{:S(2)}, u32[]{:S(2)}) collective-permute-start(bf16[512,128]{1,0:T(8,128)(2,1)S(1)} %get-tuple-element.17.refs_7_), channel_id=1, source_target_pairs={{0,12},{4,8},{8,4},{12,0},{1,13},{5,9},{9,5},{13,1},{2,14},{6,10},... | collective-permute-start | bytes 393224 | tf_op jit(solution)/shard_map/ppermute | solution.py:332
  29.0 12.1 %copy-start.10 = (f32[2048]{0:T(1024)S(1)}, f32[2048]{0:T(1024)}, u32[]{:S(2)}) copy-start(f32[2048]{0:T(1024)} %param.21) | copy-start | bytes 24580

commit v2 on v1

--- a/solution.py
+++ b/solution.py
@@ -31,10 +31,15 @@
 
 
 def spread_matrix(heads, lanes):
-    term = lax.broadcasted_iota(jnp.int32, (128, lanes), 0)
-    lane = lax.broadcasted_iota(jnp.int32, (128, lanes), 1)
-    hit = ((term % heads) == (lane // HEAD_SIZE)) & (term < 3 * heads)
-    return jnp.where(hit, 1.0, 0.0).astype(BF16)
+    term = lax.broadcasted_iota(jnp.int32, (128, 1), 0)
+    head = term
+    for k in (1, 2):
+        head = jnp.where(term >= k * heads, term - k * heads, head)
+    head = jnp.where(term >= 3 * heads, -1, head)
+    first = head * HEAD_SIZE
+    lane = lax.broadcasted_iota(jnp.int32, (1, lanes), 1)
+    hit = jnp.where(lane >= first, 1.0, 0.0) - jnp.where(lane >= first + HEAD_SIZE, 1.0, 0.0)
+    return jnp.where(head >= 0, hit, 0.0).astype(BF16)
 
 
 def stacked(v):
@@ -44,12 +49,12 @@
     return full.T.astype(BF16)
 
 
-def scan_steps(raw_ref, bias_ref, decay_ref, alive_count):
-    heads, length = raw_ref.shape
-    bias = column(bias_ref[...], heads)
-    rate = -jnp.exp(column(decay_ref[...], heads))
+def scan_steps(raw, bias_row, decay_row, alive_count):
+    heads, length = raw.shape
+    bias = column(bias_row, heads)
+    rate = -jnp.exp(column(decay_row, heads))
     position = lax.broadcasted_iota(jnp.int32, (heads, length), 1)
-    raw = raw_ref[...] + bias
+    raw = raw + bias
     soft = jnp.maximum(raw, 0.0) + jnp.log1p(jnp.exp(-jnp.abs(raw)))
     step = jnp.where(position < alive_count, soft, 0.0)
     drop = rate * step
@@ -58,65 +63,71 @@
         <= lax.broadcasted_iota(jnp.int32, (CHUNK, CHUNK), 1)
     )
     upper = jnp.where(upper, 1.0, 0.0).astype(BF16)
+    chunks = length // CHUNK
+    terms = [t for c in range(chunks) for t in split3(drop[:, c * CHUNK : (c + 1) * CHUNK])]
+    sums = jnp.dot(
+        jnp.concatenate(terms, axis=0).astype(BF16), upper, preferred_element_type=F32
+    )
     base = jnp.zeros((heads, 1), F32)
-    parts, starts = [], []
-    for c in range(length // CHUNK):
-        terms = jnp.concatenate(split3(drop[:, c * CHUNK : (c + 1) * CHUNK]), axis=0)
-        sums = jnp.dot(terms.astype(BF16), upper, preferred_element_type=F32)
-        run = sums[:heads] + sums[heads : 2 * heads] + sums[2 * heads :]
-        starts.append(base)
+    parts = []
+    for c in range(chunks):
+        i = 3 * c * heads
+        run = sums[i : i + heads] + sums[i + heads : i + 2 * heads] + sums[i + 2 * heads : i + 3 * heads]
         parts.append(run + base)
         base = base + run[:, CHUNK - 1 :]
-    return step, parts, starts, base
-
-
-def state_kernel(
-    slot_ref, length_ref, raw_ref, bias_ref, decay_ref, x_ref, b_ref, *refs, ways, dp_name
-):
-    pieces, meta_ref, spread_ref, tail_ref, bt_ref, hold = (
-        refs[:ways],
-        refs[ways],
-        refs[ways + 1],
-        refs[ways + 2],
-        refs[ways + 3],
-        refs[ways + 4],
-    )
+    return step, jnp.concatenate(parts, axis=1)
+
+
+def state_kernel(*refs, ways, dp_name, loads):
+    sources, refs = refs[:loads], refs[loads:]
+    pieces, refs = refs[:ways], refs[ways:]
+    meta_ref, spread_ref, step_ref, log_ref, *refs = refs
+    held, (tail_ref, hold, sems) = refs[:loads], refs[loads:]
+    raw_ref, bias_ref, decay_ref, length_ref, slot_ref, b_ref, x_ref = held[:7]
     heads, length = raw_ref.shape
     width = heads * HEAD_SIZE
     chan = HEAD_SIZE // ways
-    step, parts, _, end = scan_steps(raw_ref, bias_ref, decay_ref, length_ref[0])
-    logdecay = jnp.concatenate(parts, axis=1)
+    copies = [
+        pltpu.make_async_copy(source, target, sems.at[i])
+        for i, (source, target) in enumerate(zip(sources, held))
+    ]
+    for copy in copies:
+        copy.start()
+    spread_ref[...] = spread_matrix(heads, width)
+    for copy in copies[:4]:
+        copy.wait()
+    step, logdecay = scan_steps(raw_ref[...], bias_ref[...], decay_ref[...], length_ref[...])
+    step_ref[...] = step
+    log_ref[...] = logdecay
+    end = logdecay[:, length - 1 :]
     tail_ref[...] = stacked(jnp.exp(end - logdecay) * step)
-    bt_ref[...] = b_ref[...].T
-    spread_ref[...] = spread_matrix(heads, width)
     lane = lax.broadcasted_iota(jnp.int32, (8, 128), 1)
     eye = lax.broadcasted_iota(jnp.int32, (heads, 128), 0) == lax.broadcasted_iota(
         jnp.int32, (heads, 128), 1
     )
     last = jnp.sum(jnp.where(eye, jnp.exp(end), 0.0), axis=0, keepdims=True)
-    slot = slot_ref[0].astype(F32)
+    for copy in copies[4:7]:
+        copy.wait()
+    slot = slot_ref[...].astype(F32)
     meta_ref[...] = jnp.where(lane == heads, slot, jnp.broadcast_to(last, (8, 128)))
-
+    turned_b = b_ref[...].T
     per = LANES // HEAD_SIZE
-
-    def tile(t, carry):
-        at = pl.ds(pl.multiple_of(t * LANES, LANES), LANES)
+    for t in range(width // LANES):
+        at = slice(t * LANES, (t + 1) * LANES)
         scale = jnp.dot(tail_ref[...], spread_ref[:, at], preferred_element_type=F32)
         moved = (scale * x_ref[:, at].astype(F32)).astype(BF16)
-        state = jnp.dot(bt_ref[...], moved, preferred_element_type=F32)
+        state = jnp.dot(turned_b, moved, preferred_element_type=F32)
         turned = state.T.astype(BF16).reshape(per, ways, chan, 128)
-        rows = pl.ds(pl.multiple_of(t * per * chan, per * chan), per * chan)
         for d in range(ways):
-            hold[d, rows, :] = turned[:, d].reshape(per * chan, 128)
-        return carry
-
-    lax.fori_loop(0, width // LANES, tile, 0)
+            hold[d, t * per * chan : (t + 1) * per * chan, :] = turned[:, d].reshape(per * chan, 128)
     if ways == 1:
         pieces[0][...] = hold[0]
     else:
         me = lax.axis_index(dp_name)
         for k in range(ways):
             pieces[k][...] = hold[me ^ k]
+    for copy in copies[7:]:
+        copy.wait()
 
 
 def row_spread(row, heads, rows):
@@ -142,55 +153,50 @@
 
 def intra_kernel(
     after_ref,
-    length_ref,
-    raw_ref,
-    bias_ref,
-    decay_ref,
+    step_ref,
+    log_ref,
     skip_ref,
+    spread_ref,
     x_ref,
     b_ref,
     c_ref,
     y_ref,
     grow_ref,
-    spread_ref,
     in_ref,
     out_ref,
     whole_ref,
     mix_ref,
     ends_ref,
 ):
-    heads, length = raw_ref.shape
+    heads, length = step_ref.shape
     width = heads * HEAD_SIZE
     chunks = length // CHUNK
-    step, parts, starts, end = scan_steps(raw_ref, bias_ref, decay_ref, length_ref[0])
-    spread_ref[...] = spread_matrix(heads, width)
     causal = lax.broadcasted_iota(jnp.int32, (CHUNK, CHUNK), 0) >= lax.broadcasted_iota(
         jnp.int32, (CHUNK, CHUNK), 1
     )
-    ends = []
+    lane = lax.broadcasted_iota(jnp.int32, (heads, 128), 1)
+    ends = jnp.zeros((heads, 128), F32)
+    start = jnp.zeros((heads, 1), F32)
     for c in range(chunks):
         at = slice(c * CHUNK, (c + 1) * CHUNK)
-        inside = parts[c] - starts[c]
-        in_ref[at, :] = stacked(jnp.exp(-inside) * step[:, at])
+        logdecay = log_ref[:, at]
+        inside = logdecay - start
+        in_ref[at, :] = stacked(jnp.exp(-inside) * step_ref[:, at])
         out_ref[at, :] = stacked(jnp.exp(inside))
-        whole_ref[at, :] = stacked(jnp.exp(parts[c]))
-        nxt = starts[c + 1] if c + 1 < chunks else end
-        ends.append(jnp.exp(nxt - starts[c]))
+        whole_ref[at, :] = stacked(jnp.exp(logdecay))
+        ends = jnp.where(lane == c, jnp.exp(inside[:, CHUNK - 1 :]), ends)
+        start = logdecay[:, CHUNK - 1 :]
         gram = lax.dot_general(
             c_ref[at, :], b_ref[at, :], (((1,), (1,)), ((), ())), preferred_element_type=F32
         )
         mix_ref[at, :CHUNK] = jnp.where(causal, gram, 0.0).astype(BF16)
         mix_ref[at, CHUNK:] = c_ref[at, :]
-    lane = lax.broadcasted_iota(jnp.int32, (heads, 128), 1)
-    pad = jnp.zeros((heads, 128), F32)
-    for c in range(chunks):
-        pad = jnp.where(lane == c, ends[c], pad)
-    ends_ref[...] = stacked(pad)
+    ends_ref[...] = stacked(ends)
     skip_row = jnp.concatenate(split3(skip_ref[...]) + (jnp.zeros((1, 128 - 3 * heads), F32),), axis=1)
     skip_rows = jnp.broadcast_to(skip_row, (8, 128)).astype(BF16)
 
-    def tile(t, carry):
-        at = pl.ds(pl.multiple_of(t * LANES, LANES), LANES)
+    for t in range(width // LANES):
+        at = slice(t * LANES, (t + 1) * LANES)
         hot = spread_ref[:, at]
         skip = jnp.dot(skip_rows, hot, preferred_element_type=F32)[0:1]
         decay = jnp.dot(ends_ref[0:8, :], hot, preferred_element_type=F32)
@@ -210,40 +216,37 @@
                     b_ref[rows, :], moved, (((0,), (0,)), ((), ())), preferred_element_type=F32
                 )
                 state = decay[c : c + 1] * (state + fresh)
-        return carry
-
-    lax.fori_loop(0, width // LANES, tile, 0)
-
-
-def norm_kernel(length_ref, offset_ref, *refs, ways, dp_name, heads, block):
-    pieces = refs[:ways]
-    y_ref, grow_ref, c_ref, gain_ref, mixed_ref, hold = refs[ways:]
+
+
+def norm_kernel(*refs, ways, dp_name, heads, block):
+    pieces, refs = refs[:ways], refs[ways:]
+    length_ref, offset_ref, y_ref, grow_ref, c_ref, gain_ref, mixed_ref, hold, done, sems = refs
     chan = HEAD_SIZE // ways
-    i = pl.program_id(0)
-
-    @pl.when(i == 0)
-    def _():
-        if ways == 1:
-            hold[...] = pieces[0][...]
-        else:
-            me = lax.axis_index(dp_name)
-            for k in range(ways):
-                start = pl.multiple_of((me ^ k) * chan, chan)
-                for h in range(heads):
-                    hold[pl.ds(h * HEAD_SIZE + start, chan), :] = pieces[k][
-                        h * chan : (h + 1) * chan, :
-                    ]
-
-    rows = pl.ds(pl.multiple_of(i * block, block), block)
-    carried = lax.dot_general(
-        c_ref[rows, :], hold[...], (((1,), (1,)), ((), ())), preferred_element_type=F32
-    )
-    scan = y_ref[rows, :] + grow_ref[rows, :] * carried
-    meansq = jnp.mean(scan * scan, axis=1, keepdims=True)
-    position = lax.broadcasted_iota(jnp.int32, (block, 1), 0) + i * block
-    keep = (position < length_ref[0]) & (position >= offset_ref[0])
-    factor = jnp.where(keep, lax.rsqrt(meansq + 1e-05), 0.0)
-    mixed_ref[0] = (scan * factor * gain_ref[...]).astype(BF16)
+    if ways == 1:
+        hold[...] = pieces[0][...]
+    else:
+        me = lax.axis_index(dp_name)
+        for k in range(ways):
+            start = pl.multiple_of((me ^ k) * chan, chan)
+            for h in range(heads):
+                hold[pl.ds(h * HEAD_SIZE + start, chan), :] = pieces[k][h * chan : (h + 1) * chan, :]
+    position = lax.broadcasted_iota(jnp.int32, (block, 1), 0)
+    copies = []
+    for i in range(y_ref.shape[0] // block):
+        rows = slice(i * block, (i + 1) * block)
+        carried = lax.dot_general(
+            c_ref[rows, :], hold[...], (((1,), (1,)), ((), ())), preferred_element_type=F32
+        )
+        scan = y_ref[rows, :] + grow_ref[rows, :] * carried
+        meansq = jnp.mean(scan * scan, axis=1, keepdims=True)
+        keep = (position + i * block < length_ref[...]) & (position + i * block >= offset_ref[...])
+        factor = jnp.where(keep, lax.rsqrt(meansq + 1e-05), 0.0)
+        done[rows, :] = (scan * factor * gain_ref[...]).astype(BF16)
+        copy = pltpu.make_async_copy(done.at[rows, :], mixed_ref.at[0, rows, :], sems.at[i])
+        copy.start()
+        copies.append(copy)
+    for copy in copies:
+        copy.wait()
 
 
 def final_kernel(*refs, ways, dp_name, heads):
@@ -286,35 +289,55 @@
     direct = dp in (2, 4)
     ways = dp if direct else 1
     rows = heads * HEAD_SIZE // ways
-    x, b, c, raw = ssm_input[0], input_proj[0], output_proj[0], step_raw[0]
-    bias, decay, skip = step_bias[None], decay_log[None], skip_gain[None]
     piece = jax.ShapeDtypeStruct((rows, state), BF16)
     params = pltpu.CompilerParams(vmem_limit_bytes=24 << 20)
-
-    *local_parts, meta = pl.pallas_call(
-        functools.partial(state_kernel, ways=ways, dp_name="dp"),
-        out_shape=[piece] * ways + [jax.ShapeDtypeStruct((8, 128), F32)],
-        in_specs=[SMEM, SMEM] + [VMEM] * 5,
-        out_specs=[VMEM] * (ways + 1),
+    loaded = [
+        step_raw[0],
+        step_bias[None],
+        decay_log[None],
+        row_lengths[None],
+        slot_ids[None],
+        input_proj[0],
+        ssm_input[0],
+        output_proj[0],
+        skip_gain[None],
+        norm_gain[None],
+        row_offsets[None],
+        template_state.reshape(-1, state),
+        slot_decay,
+    ]
+    shape_of = lambda v: jax.ShapeDtypeStruct(v.shape, v.dtype)
+    outs = pl.pallas_call(
+        functools.partial(state_kernel, ways=ways, dp_name="dp", loads=len(loaded)),
+        out_shape=[piece] * ways
+        + [
+            jax.ShapeDtypeStruct((8, 128), F32),
+            jax.ShapeDtypeStruct((128, width), BF16),
+            jax.ShapeDtypeStruct((heads, length), F32),
+            jax.ShapeDtypeStruct((heads, length), F32),
+        ]
+        + [shape_of(v) for v in loaded],
+        in_specs=[pl.BlockSpec(memory_space=pltpu.HBM)] * len(loaded),
+        out_specs=[VMEM] * (ways + 4 + len(loaded)),
         scratch_shapes=[
-            pltpu.VMEM((128, width), BF16),
             pltpu.VMEM((length, 128), BF16),
-            pltpu.VMEM((128, length), BF16),
             pltpu.VMEM((ways, rows, state), BF16),
+            pltpu.SemaphoreType.DMA((len(loaded),)),
         ],
         compiler_params=params,
         cost_estimate=cost(2 * length * width * 256, 3 << 20),
         name="state",
-    )(slot_ids, row_lengths, raw, bias, decay, x, b)
+    )(*loaded)
+    local_parts, (meta, spread, step, logdecay, *held) = outs[:ways], outs[ways:]
+    _, _, _, alive, _, b, x, c, skip, gain, offset, template, decays = held
 
     def intra(after):
         return pl.pallas_call(
             intra_kernel,
             out_shape=[jax.ShapeDtypeStruct((length, width), F32)] * 2,
-            in_specs=[VMEM, SMEM] + [VMEM] * 7,
+            in_specs=[VMEM] * 8,
             out_specs=[VMEM] * 2,
             scratch_shapes=[
-                pltpu.VMEM((128, width), BF16),
                 pltpu.VMEM((length, 128), BF16),
                 pltpu.VMEM((length, 128), BF16),
                 pltpu.VMEM((length, 128), BF16),
@@ -324,7 +347,7 @@
             compiler_params=params,
             cost_estimate=cost(2 * length * width * 1024, 16 << 20),
             name="intra",
-        )(after, row_lengths, raw, bias, decay, skip, x, b, c)
+        )(after, step, logdecay, skip, spread, x, b, c)
 
     if direct:
 
@@ -346,8 +369,8 @@
         )(
             *metas,
             cache_states.reshape(slots, rows, state),
-            slot_decay,
-            template_state.reshape(rows, state),
+            decays,
+            template,
         )
         sent = {k: swap(resumed[k], k) for k in order}
         y, grow = intra(resumed[0][:8, :])
@@ -387,14 +410,17 @@
     mixed = pl.pallas_call(
         functools.partial(norm_kernel, ways=ways, dp_name="dp", heads=heads, block=block),
         out_shape=jax.ShapeDtypeStruct((1, length, width), BF16),
-        grid=(length // block,),
-        in_specs=[SMEM, SMEM] + [VMEM] * (ways + 4),
-        out_specs=pl.BlockSpec((1, block, width), lambda i: (0, i, 0)),
-        scratch_shapes=[pltpu.VMEM((heads * HEAD_SIZE, state), BF16)],
+        in_specs=[VMEM] * (ways + 6),
+        out_specs=pl.BlockSpec(memory_space=pltpu.HBM),
+        scratch_shapes=[
+            pltpu.VMEM((heads * HEAD_SIZE, state), BF16),
+            pltpu.VMEM((length, width), BF16),
+            pltpu.SemaphoreType.DMA((length // block,)),
+        ],
         compiler_params=params,
         cost_estimate=cost(2 * length * width * 128, 4 << 20),
         name="norm",
-    )(row_lengths, row_offsets, *arrived, y, grow, c, norm_gain[None])
+    )(*arrived, alive, offset, y, grow, c, gain)
     return (mixed, new_states)
 
 

time: 44.6 us -> 50.1 us (1.12)
  waiting for transfers between devices: 1.77 us -> 4.88 us
  local copies, waits for them, and re-layouts: 6.27 us -> 8.5 us
  starting transfers between devices: 14.8 us -> 15.4 us
    ppermute x9, waiting for transfers between devices: 1.77 us -> 4.88 us  [swap(): return lax.ppermute(v, 'dp', [(i, i ^ k) for i in range(dp)])]
    unnamed x28 -> x22, local copies, waits for them, and re-layouts: 6.26 us -> 8.49 us
    pallas_call x1, Pallas kernels: 9.3 us -> 7.87 us  [intra(): pl.pallas_call(intra_kernel, out_shape=[jax.ShapeDtypeStruct((length, wid...]
    pallas_call x1, Pallas kernels: 3.17 us -> 3.89 us  [local(): pl.pallas_call(functools.partial(norm_kernel, ways=ways, dp_name='dp', he...]
    ppermute x9, starting transfers between devices: 14.8 us -> 15.4 us  [swap(): return lax.ppermute(v, 'dp', [(i, i ^ k) for i in range(dp)])]
  transfers between devices with their start and end apart: 9 -> 9, of which waited for: 2 -> 3; matrix products, arithmetic and copies ran while one was open for 0% -> 0% of each run, Pallas kernels for 25% -> 19%
where the time goes in v2:
time: 50.1 us; the launch traced here: 49.7 us
  Pallas kernels  18.3 us (37%)
  starting transfers between devices  15.4 us (31%)
  local copies, waits for them, and re-layouts  8.5 us (17%)
  waiting for transfers between devices  4.88 us (10%)
  between operations  2.63 us (5%)
    ppermute x9, starting transfers between devices, swap(): return lax.ppermute(v, 'dp', [(i, i ^ k) for i in range(dp)])  15.4 us
    unnamed x22, local copies, waits for them, and re-layouts  8.49 us
    pallas_call x1, Pallas kernels, intra(): pl.pallas_call(intra_kernel, out_shape=[jax.ShapeDtypeStruct((length, wid...  7.87 us
    ppermute x9, waiting for transfers between devices, swap(): return lax.ppermute(v, 'dp', [(i, i ^ k) for i in range(dp)])  4.88 us
    pallas_call x1, Pallas kernels, local(): pl.pallas_call(functools.partial(state_kernel, ways=ways, dp_name='dp', l...  4.79 us
    pallas_call x1, Pallas kernels, local(): pl.pallas_call(functools.partial(norm_kernel, ways=ways, dp_name='dp', he...  3.89 us
    pallas_call x1, Pallas kernels, local(): pl.pallas_call(functools.partial(final_kernel, ways=dp, dp_name='dp', hea...  1.22 us
  transfers between devices with their start and end apart: 9, of which 3 were waited for; matrix products, arithmetic and copies ran while one was open for 0% of the time, Pallas kernels for 19%

profile of v2, /device:TPU:0, one launch (start us, length us, event | category | flops | bytes accessed | tf_op | source)
XLA Modules:
  0.0 49.7 jit_solution(1676863698855378603)
XLA Ops:
  2.6 0.0 copy-start
  2.6 1.6 %copy-done = bf16[1,512,2048]{2,1,0:T(8,128)(2,1)S(1)} copy-done((bf16[1,512,2048]{2,1,0:T(8,128)(2,1)S(1)}, bf16[1,512,2048]{2,1,0:T(8,128)(2,1)}, u32[]{:S(2)}) %copy-start) | copy-done | bytes 2097176
  4.2 0.0 copy-start.2
  4.2 0.9 %copy-done.2 = bf16[1,512,128]{2,1,0:T(8,128)(2,1)S(1)} copy-done((bf16[1,512,128]{2,1,0:T(8,128)(2,1)S(1)}, bf16[1,512,128]{2,1,0:T(8,128)(2,1)}, u32[]{:S(2)}) %copy-start.2) | copy-done | bytes 131096
  5.1 0.0 copy-start.3
  5.1 0.9 %copy-done.3 = bf16[1,512,128]{2,1,0:T(8,128)(2,1)S(1)} copy-done((bf16[1,512,128]{2,1,0:T(8,128)(2,1)S(1)}, bf16[1,512,128]{2,1,0:T(8,128)(2,1)}, u32[]{:S(2)}) %copy-start.3) | copy-done | bytes 131096
  6.0 0.0 copy-start.4
  6.0 0.9 %copy-done.4 = bf16[32,16,128]{2,1,0:T(8,128)(2,1)S(1)} copy-done((bf16[32,16,128]{2,1,0:T(8,128)(2,1)S(1)}, bf16[32,16,128]{2,1,0:T(8,128)(2,1)}, u32[]{:S(2)}) %copy-start.4) | copy-done | bytes 131096
  6.9 0.0 copy-start.5
  6.9 0.8 %copy-done.5 = f32[1,32,512]{2,1,0:T(8,128)S(1)} copy-done((f32[1,32,512]{2,1,0:T(8,128)S(1)}, f32[1,32,512]{2,1,0:T(8,128)}, u32[]{:S(2)}) %copy-start.5) | copy-done | bytes 65560
  7.7 0.0 copy-start.6
  7.7 0.7 %copy-done.6 = f32[2048]{0:T(1024)S(1)} copy-done((f32[2048]{0:T(1024)S(1)}, f32[2048]{0:T(1024)}, u32[]{:S(2)}) %copy-start.6) | copy-done | bytes 8216
  8.4 0.0 copy-start.7
  8.4 0.7 %copy-done.7 = f32[16,32]{1,0:T(8,128)S(1)} copy-done((f32[16,32]{1,0:T(8,128)S(1)}, f32[16,32]{1,0:T(8,128)}, u32[]{:S(2)}) %copy-start.7) | copy-done | bytes 2072
  9.1 0.0 copy-start.8
  9.1 0.7 %copy-done.8 = f32[32]{0:T(128)S(1)} copy-done((f32[32]{0:T(128)S(1)}, f32[32]{0:T(128)}, u32[]{:S(2)}) %copy-start.8) | copy-done | bytes 152
  9.8 0.0 copy-start.9
  9.8 0.7 %copy-done.9 = f32[32]{0:T(128)S(1)} copy-done((f32[32]{0:T(128)S(1)}, f32[32]{0:T(128)}, u32[]{:S(2)}) %copy-start.9) | copy-done | bytes 152
  10.4 0.0 copy-start.10
  10.4 0.7 %copy-done.10 = f32[32]{0:T(128)S(1)} copy-done((f32[32]{0:T(128)S(1)}, f32[32]{0:T(128)}, u32[]{:S(2)}) %copy-start.10) | copy-done | bytes 152
  11.1 0.0 copy-start.1
  11.1 4.8 %state.1 = (bf16[512,128]{1,0:T(8,128)(2,1)S(1)}, bf16[512,128]{1,0:T(8,128)(2,1)S(1)}, bf16[512,128]{1,0:T(8,128)(2,1)S(1)}, bf16[512,128]{1,0:T(8,128)(2,1)S(1...) custom-call(f32[32,512]{1,0:T(8,128)S(1)} %bitcast.22, ...), custom_call_target="tpu_custom_call" | custom-call | flops 536870912 | bytes 3145728 | tf_op jit(solution)/shard_map/state/pallas_call | solution.py:310
  15.9 3.1 %collective-permute-start.6 = (bf16[512,128]{1,0:T(8,128)(2,1)S(1)}, bf16[512,128]{1,0:T(8,128)(2,1)S(1)}, u32[]{:S(2)}, u32[]{:S(2)}) collective-permute-start(bf16[512,128]{1,0:T(8,128)(2,1)S(1)} %get-tuple-element.45), channel_id=1, source_target_pairs={{0,4},{4,0},{8,12},{12,8},{1,5},{5,1},{9,13},{13,9},{2,6},{6,2},{1... | collective-permute-start | bytes 393224 | tf_op jit(solution)/shard_map/ppermute | solution.py:355
  19.0 2.5 %collective-permute-start.2 = (f32[8,128]{1,0:T(8,128)S(1)}, f32[8,128]{1,0:T(8,128)S(1)}, u32[]{:S(2)}, u32[]{:S(2)}) collective-permute-start(f32[8,128]{1,0:T(8,128)S(1)} %get-tuple-element.25.refs_0_.refs_8_), channel_id=1, source_target_pairs={{0,12},{4,8},{8,4},{12,0},{1,13},{5,9},{9,5},{13,1},{2,14},{6,10},... | collective-permute-start | bytes 12296 | tf_op jit(solution)/shard_map/ppermute | solution.py:355
  21.5 0.1 collective-permute-start.1
  21.6 1.8 %collective-permute-start = (f32[8,128]{1,0:T(8,128)S(1)}, f32[8,128]{1,0:T(8,128)S(1)}, u32[]{:S(2)}, u32[]{:S(2)}) collective-permute-start(f32[8,128]{1,0:T(8,128)S(1)} %get-tuple-element.25.refs_0_.refs_8_), channel_id=1, source_target_pairs={{0,4},{4,0},{8,12},{12,8},{1,5},{5,1},{9,13},{13,9},{2,6},{6,2},{1... | collective-permute-start | bytes 12296 | tf_op jit(solution)/shard_map/ppermute | solution.py:355
  23.4 1.7 %collective-permute-start.7 = (bf16[512,128]{1,0:T(8,128)(2,1)S(1)}, bf16[512,128]{1,0:T(8,128)(2,1)S(1)}, u32[]{:S(2)}, u32[]{:S(2)}) collective-permute-start(bf16[512,128]{1,0:T(8,128)(2,1)S(1)} %get-tuple-element.46), channel_id=1, source_target_pairs={{0,8},{4,12},{8,0},{12,4},{1,9},{5,13},{9,1},{13,5},{2,10},{6,14},... | collective-permute-start | bytes 393224 | tf_op jit(solution)/shard_map/ppermute | solution.py:355
  25.1 0.0 collective-permute-done.2.refs_3_.refs_11_
  25.1 1.8 %collective-permute-start.8 = (bf16[512,128]{1,0:T(8,128)(2,1)S(1)}, bf16[512,128]{1,0:T(8,128)(2,1)S(1)}, u32[]{:S(2)}, u32[]{:S(2)}) collective-permute-start(bf16[512,128]{1,0:T(8,128)(2,1)S(1)} %get-tuple-element.47), channel_id=1, source_target_pairs={{0,12},{4,8},{8,4},{12,0},{1,13},{5,9},{9,5},{13,1},{2,14},{6,10},... | collective-permute-start | bytes 393224 | tf_op jit(solution)/shard_map/ppermute | solution.py:355
  26.9 0.2 collective-permute-done.1.refs_2_.refs_10_
  27.1 0.0 collective-permute-done.refs_1_.refs_9_
  27.1 0.0 copy-done.1
  27.1 0.5 %resume.1 = (bf16[512,128]{1,0:T(8,128)(2,1)S(1)}, bf16[512,128]{1,0:T(8,128)(2,1)S(1)}, bf16[512,128]{1,0:T(8,128)(2,1)S(1)}, bf16[512,128]{1,0:T(8,128)(2,1)S(1)}) custom-call(f32[8,128]{1,0:T(8,128)S(1)} %get-tuple-element.25.refs_0_.refs_8_, f32[8,128]{1,0:T(8,128)S(1)} %collective-permute-done.refs_1_.refs_9_, ...), custom_call_target="tpu_custom_call" | custom-call | flops 67108864 | bytes 2097152 | tf_op jit(solution)/shard_map/resume/pallas_call | solution.py:361
  27.7 0.1 collective-permute-start.3
  27.7 2.4 %collective-permute-start.4 = (bf16[512,128]{1,0:T(8,128)(2,1)S(1)}, bf16[512,128]{1,0:T(8,128)(2,1)S(1)}, u32[]{:S(2)}, u32[]{:S(2)}) collective-permute-start(bf16[512,128]{1,0:T(8,128)(2,1)S(1)} %get-tuple-element.30.refs_6_), channel_id=1, source_target_pairs={{0,8},{4,12},{8,0},{12,4},{1,9},{5,13},{9,1},{13,5},{2,10},{6,14},... | collective-permute-start | bytes 393224 | tf_op jit(solution)/shard_map/ppermute | solution.py:355
  30.1 0.0 collective-permute-done.6.refs_1_
  30.1 2.0 %collective-permute-start.5 = (bf16[512,128]{1,0:T(8,128)(2,1)S(1)}, bf16[512,128]{1,0:T(8,128)(2,1)S(1)}, u32[]{:S(2)}, u32[]{:S(2)}) collective-permute-start(bf16[512,128]{1,0:T(8,128)(2,1)S(1)} %get-tuple-element.31.refs_7_), channel_id=1, source_target_pairs={{0,12},{4,8},{8,4},{12,0},{1,13},{5,9},{9,5},{13,1},{2,14},{6,10},... | collective-permute-start | bytes 393224 | tf_op jit(solution)/shard_map/ppermute | solution.py:355
  32.1 7.9 %intra.1 = (f32[512,2048]{1,0:T(8,128)S(1)}, f32[512,2048]{1,0:T(8,128)S(1)}) custom-call(bf16[8,128]{1,0:T(8,128)(2,1)S(1)} %slice.3.after_ref, f32[32,512]{1,0:T(8,128)S(1)} %get-tuple-element.34.step_ref, f32[32,512]{1,0:T(8,128)S(1)} %get-tuple-element.35.log_ref, f32[1,32]{1,0:T(1,128)S(1)} %get-tuple-element.36.skip_ref, ...), custom_call_target="tpu_custom_call" | custom-call | flops 2147483648 | bytes 16777216 | tf_op jit(solution)/shard_map/intra/pallas_call | solution.py:335
  40.0 0.2 collective-permute-done.7.refs_2_
  40.2 0.0 collective-permute-done.8.refs_3_
  40.2 1.2 %final.1 = bf16[4,512,128]{2,1,0:T(8,128)(2,1)} custom-call(bf16[512,128]{1,0:T(8,128)(2,1)S(1)} %get-tuple-element.44.refs_0_, bf16[512,128]{1,0:T(8,128)(2,1)S(1)} %collective-permute-done.6.refs_1_, bf16[512,128]{1,0:T(8,128)(2,1)S(1)} %collective-permute-done.7.refs_2_, bf16[512,128]{1,0:T(8,128)(2,1)S(1)} %collective-permute-done.8.refs_3_, ...), custom_call_target="tpu_custom_call" | custom-call | flops 67108864 | bytes 2097152 | tf_op jit(solution)/shard_map/final/pallas_call | solution.py:377
  41.4 0.0 collective-permute-done.3.refs_1_
  41.4 4.4 %collective-permute-done.4.refs_2_ = bf16[512,128]{1,0:T(8,128)(2,1)S(1)} collective-permute-done((bf16[512,128]{1,0:T(8,128)(2,1)S(1)}, bf16[512,128]{1,0:T(8,128)(2,1)S(1)}, u32[]{:S(2)}, u32[]{:S(2)}) %collective-permute-start.4) | collective-permute-done | bytes 131104 | tf_op jit(solution)/shard_map/ppermute | solution.py:355
  45.8 0.0 collective-permute-done.5.refs_3_
  45.8 3.9 %norm.1 = bf16[1,512,2048]{2,1,0:T(8,128)(2,1)} custom-call(bf16[512,128]{1,0:T(8,128)(2,1)S(1)} %get-tuple-element.28.refs_0_.refs_4_, bf16[512,128]{1,0:T(8,128)(2,1)S(1)} %collective-permute-done.3.refs_1_, bf16[512,128]{1,0:T(8,128)(2,1)S(1)} %collective-permute-done.4.refs_2_, bf16[512,128]{1,0:T(8,128)(2,1)S(1)} %collective-permute-done.5.refs_3_, ...), custom_call_target="tpu_custom_call" | custom-call | flops 268435456 | bytes 4194304 | tf_op jit(solution)/shard_map/norm/pallas_call | solution.py:410
  (1 shorter events, 0.0 us)
Async XLA Ops:
  2.6 1.6 %copy-start = (bf16[1,512,2048]{2,1,0:T(8,128)(2,1)S(1)}, bf16[1,512,2048]{2,1,0:T(8,128)(2,1)}, u32[]{:S(2)}) copy-start(bf16[1,512,2048]{2,1,0:T(8,128)(2,1)} %param.14) | copy-start | bytes 6291460
  4.2 0.9 %copy-start.2 = (bf16[1,512,128]{2,1,0:T(8,128)(2,1)S(1)}, bf16[1,512,128]{2,1,0:T(8,128)(2,1)}, u32[]{:S(2)}) copy-start(bf16[1,512,128]{2,1,0:T(8,128)(2,1)} %param.15) | copy-start | bytes 393220
  5.1 0.9 %copy-start.3 = (bf16[1,512,128]{2,1,0:T(8,128)(2,1)S(1)}, bf16[1,512,128]{2,1,0:T(8,128)(2,1)}, u32[]{:S(2)}) copy-start(bf16[1,512,128]{2,1,0:T(8,128)(2,1)} %param.16) | copy-start | bytes 393220
  6.0 0.9 %copy-start.4 = (bf16[32,16,128]{2,1,0:T(8,128)(2,1)S(1)}, bf16[32,16,128]{2,1,0:T(8,128)(2,1)}, u32[]{:S(2)}) copy-start(bf16[32,16,128]{2,1,0:T(8,128)(2,1)} %param.24) | copy-start | bytes 393220
  6.9 0.8 %copy-start.5 = (f32[1,32,512]{2,1,0:T(8,128)S(1)}, f32[1,32,512]{2,1,0:T(8,128)}, u32[]{:S(2)}) copy-start(f32[1,32,512]{2,1,0:T(8,128)} %param.17) | copy-start | bytes 196612
  7.7 0.7 %copy-start.6 = (f32[2048]{0:T(1024)S(1)}, f32[2048]{0:T(1024)}, u32[]{:S(2)}) copy-start(f32[2048]{0:T(1024)} %param.21) | copy-start | bytes 24580
  8.4 0.7 %copy-start.7 = (f32[16,32]{1,0:T(8,128)S(1)}, f32[16,32]{1,0:T(8,128)}, u32[]{:S(2)}) copy-start(f32[16,32]{1,0:T(8,128)} %refs_12_.1) | copy-start | bytes 6148
  9.1 0.7 %copy-start.8 = (f32[32]{0:T(128)S(1)}, f32[32]{0:T(128)}, u32[]{:S(2)}) copy-start(f32[32]{0:T(128)} %param.18) | copy-start | bytes 388
  9.8 0.7 %copy-start.9 = (f32[32]{0:T(128)S(1)}, f32[32]{0:T(128)}, u32[]{:S(2)}) copy-start(f32[32]{0:T(128)} %param.19) | copy-start | bytes 388
  10.4 0.7 %copy-start.10 = (f32[32]{0:T(128)S(1)}, f32[32]{0:T(128)}, u32[]{:S(2)}) copy-start(f32[32]{0:T(128)} %param.20) | copy-start | bytes 388
  11.1 16.1 %copy-start.1 = (bf16[16,32,16,128]{3,2,1,0:T(8,128)(2,1)S(1)}, bf16[16,32,16,128]{3,2,1,0:T(8,128)(2,1)}, u32[]{:S(2)}) copy-start(bf16[16,32,16,128]{3,2,1,0:T(8,128)(2,1)} %param.22) | copy-start | bytes 6291460
  15.9 14.2 %collective-permute-start.6 = (bf16[512,128]{1,0:T(8,128)(2,1)S(1)}, bf16[512,128]{1,0:T(8,128)(2,1)S(1)}, u32[]{:S(2)}, u32[]{:S(2)}) collective-permute-start(bf16[512,128]{1,0:T(8,128)(2,1)S(1)} %get-tuple-element.45), channel_id=1, source_target_pairs={{0,4},{4,0},{8,12},{12,8},{1,5},{5,1},{9,13},{13,9},{2,6},{6,2},{1... | collective-permute-start | bytes 393224 | tf_op jit(solution)/shard_map/ppermute | solution.py:355
  19.0 6.1 %collective-permute-start.2 = (f32[8,128]{1,0:T(8,128)S(1)}, f32[8,128]{1,0:T(8,128)S(1)}, u32[]{:S(2)}, u32[]{:S(2)}) collective-permute-start(f32[8,128]{1,0:T(8,128)S(1)} %get-tuple-element.25.refs_0_.refs_8_), channel_id=1, source_target_pairs={{0,12},{4,8},{8,4},{12,0},{1,13},{5,9},{9,5},{13,1},{2,14},{6,10},... | collective-permute-start | bytes 12296 | tf_op jit(solution)/shard_map/ppermute | solution.py:355
  21.5 5.7 %collective-permute-start.1 = (f32[8,128]{1,0:T(8,128)S(1)}, f32[8,128]{1,0:T(8,128)S(1)}, u32[]{:S(2)}, u32[]{:S(2)}) collective-permute-start(f32[8,128]{1,0:T(8,128)S(1)} %get-tuple-element.25.refs_0_.refs_8_), channel_id=1, source_target_pairs={{0,8},{4,12},{8,0},{12,4},{1,9},{5,13},{9,1},{13,5},{2,10},{6,14},... | collective-permute-start | bytes 12296 | tf_op jit(solution)/shard_map/ppermute | solution.py:355
  21.6 5.5 %collective-permute-start = (f32[8,128]{1,0:T(8,128)S(1)}, f32[8,128]{1,0:T(8,128)S(1)}, u32[]{:S(2)}, u32[]{:S(2)}) collective-permute-start(f32[8,128]{1,0:T(8,128)S(1)} %get-tuple-element.25.refs_0_.refs_8_), channel_id=1, source_target_pairs={{0,4},{4,0},{8,12},{12,8},{1,5},{5,1},{9,13},{13,9},{2,6},{6,2},{1... | collective-permute-start | bytes 12296 | tf_op jit(solution)/shard_map/ppermute | solution.py:355
  23.4 16.8 %collective-permute-start.7 = (bf16[512,128]{1,0:T(8,128)(2,1)S(1)}, bf16[512,128]{1,0:T(8,128)(2,1)S(1)}, u32[]{:S(2)}, u32[]{:S(2)}) collective-permute-start(bf16[512,128]{1,0:T(8,128)(2,1)S(1)} %get-tuple-element.46), channel_id=1, source_target_pairs={{0,8},{4,12},{8,0},{12,4},{1,9},{5,13},{9,1},{13,5},{2,10},{6,14},... | collective-permute-start | bytes 393224 | tf_op jit(solution)/shard_map/ppermute | solution.py:355
  25.1 15.1 %collective-permute-start.8 = (bf16[512,128]{1,0:T(8,128)(2,1)S(1)}, bf16[512,128]{1,0:T(8,128)(2,1)S(1)}, u32[]{:S(2)}, u32[]{:S(2)}) collective-permute-start(bf16[512,128]{1,0:T(8,128)(2,1)S(1)} %get-tuple-element.47), channel_id=1, source_target_pairs={{0,12},{4,8},{8,4},{12,0},{1,13},{5,9},{9,5},{13,1},{2,14},{6,10},... | collective-permute-start | bytes 393224 | tf_op jit(solution)/shard_map/ppermute | solution.py:355
  27.7 13.8 %collective-permute-start.3 = (bf16[512,128]{1,0:T(8,128)(2,1)S(1)}, bf16[512,128]{1,0:T(8,128)(2,1)S(1)}, u32[]{:S(2)}, u32[]{:S(2)}) collective-permute-start(bf16[512,128]{1,0:T(8,128)(2,1)S(1)} %get-tuple-element.29.refs_5_), channel_id=1, source_target_pairs={{0,4},{4,0},{8,12},{12,8},{1,5},{5,1},{9,13},{13,9},{2,6},{6,2},{1... | collective-permute-start | bytes 393224 | tf_op jit(solution)/shard_map/ppermute | solution.py:355
  27.7 18.1 %collective-permute-start.4 = (bf16[512,128]{1,0:T(8,128)(2,1)S(1)}, bf16[512,128]{1,0:T(8,128)(2,1)S(1)}, u32[]{:S(2)}, u32[]{:S(2)}) collective-permute-start(bf16[512,128]{1,0:T(8,128)(2,1)S(1)} %get-tuple-element.30.refs_6_), channel_id=1, source_target_pairs={{0,8},{4,12},{8,0},{12,4},{1,9},{5,13},{9,1},{13,5},{2,10},{6,14},... | collective-permute-start | bytes 393224 | tf_op jit(solution)/shard_map/ppermute | solution.py:355
  30.1 15.7 %collective-permute-start.5 = (bf16[512,128]{1,0:T(8,128)(2,1)S(1)}, bf16[512,128]{1,0:T(8,128)(2,1)S(1)}, u32[]{:S(2)}, u32[]{:S(2)}) collective-permute-start(bf16[512,128]{1,0:T(8,128)(2,1)S(1)} %get-tuple-element.31.refs_7_), channel_id=1, source_target_pairs={{0,12},{4,8},{8,4},{12,0},{1,13},{5,9},{9,5},{13,1},{2,14},{6,10},... | collective-permute-start | bytes 393224 | tf_op jit(solution)/shard_map/ppermute | solution.py:355

commit v3 on v2

--- a/solution.py
+++ b/solution.py
@@ -259,6 +259,10 @@
         out_ref[me ^ k] = (
             pieces[k][...].astype(F32) + whole * resumed[k][...].astype(F32)
         ).astype(BF16)
+
+
+def pinned(v):
+    return v if v.dtype == jnp.int32 else pltpu.with_memory_space_constraint(v, pltpu.HBM)
 
 
 def cost(flops, size):
@@ -327,7 +331,7 @@
         compiler_params=params,
         cost_estimate=cost(2 * length * width * 256, 3 << 20),
         name="state",
-    )(*loaded)
+    )(*[pinned(v) for v in loaded])
     local_parts, (meta, spread, step, logdecay, *held) = outs[:ways], outs[ways:]
     _, _, _, alive, _, b, x, c, skip, gain, offset, template, decays = held
 

time: 50.1 us -> 41.9 us (0.84)
  local copies, waits for them, and re-layouts: 8.5 us -> 0.01 us
    unnamed x22 -> x2, local copies, waits for them, and re-layouts: 8.49 us -> 0.01 us
  transfers between devices with their start and end apart: 9 -> 9, of which waited for: 3 -> 3; matrix products, arithmetic and copies ran while one was open for 0% -> 0% of each run, Pallas kernels for 19% -> 23%
where the time goes in v3:
time: 41.9 us; the launch traced here: 41.7 us
  Pallas kernels  18.6 us (44%)
  starting transfers between devices  15.4 us (37%)
  waiting for transfers between devices  4.89 us (12%)
  between operations  2.77 us (7%)
    ppermute x9, starting transfers between devices, swap(): return lax.ppermute(v, 'dp', [(i, i ^ k) for i in range(dp)])  15.4 us
    pallas_call x1, Pallas kernels, intra(): pl.pallas_call(intra_kernel, out_shape=[jax.ShapeDtypeStruct((length, wid...  7.86 us
    pallas_call x1, Pallas kernels, local(): pl.pallas_call(functools.partial(state_kernel, ways=ways, dp_name='dp', l...  5.1 us
    ppermute x9, waiting for transfers between devices, swap(): return lax.ppermute(v, 'dp', [(i, i ^ k) for i in range(dp)])  4.89 us
    pallas_call x1, Pallas kernels, local(): pl.pallas_call(functools.partial(norm_kernel, ways=ways, dp_name='dp', he...  3.95 us
    pallas_call x1, Pallas kernels, local(): pl.pallas_call(functools.partial(final_kernel, ways=dp, dp_name='dp', hea...  1.22 us
  transfers between devices with their start and end apart: 9, of which 3 were waited for; matrix products, arithmetic and copies ran while one was open for 0% of the time, Pallas kernels for 23%

profile of v3, /device:TPU:0, one launch (start us, length us, event | category | flops | bytes accessed | tf_op | source)
XLA Modules:
  0.0 41.7 jit_solution(14672428069955947128)
XLA Ops:
  0.6 0.0 copy-start
  2.7 5.1 %state.1 = (bf16[512,128]{1,0:T(8,128)(2,1)S(1)}, bf16[512,128]{1,0:T(8,128)(2,1)S(1)}, bf16[512,128]{1,0:T(8,128)(2,1)S(1)}, bf16[512,128]{1,0:T(8,128)(2,1)S(1...) custom-call(f32[32,512]{1,0:T(8,128)} %bitcast.23, ...), custom_call_target="tpu_custom_call" | custom-call | flops 536870912 | bytes 3145728 | tf_op jit(solution)/shard_map/state/pallas_call | solution.py:314
  7.8 3.1 %collective-permute-start.6 = (bf16[512,128]{1,0:T(8,128)(2,1)S(1)}, bf16[512,128]{1,0:T(8,128)(2,1)S(1)}, u32[]{:S(2)}, u32[]{:S(2)}) collective-permute-start(bf16[512,128]{1,0:T(8,128)(2,1)S(1)} %get-tuple-element.45), channel_id=1, source_target_pairs={{0,4},{4,0},{8,12},{12,8},{1,5},{5,1},{9,13},{13,9},{2,6},{6,2},{1... | collective-permute-start | bytes 393224 | tf_op jit(solution)/shard_map/ppermute | solution.py:359
  11.0 2.5 %collective-permute-start.2 = (f32[8,128]{1,0:T(8,128)S(1)}, f32[8,128]{1,0:T(8,128)S(1)}, u32[]{:S(2)}, u32[]{:S(2)}) collective-permute-start(f32[8,128]{1,0:T(8,128)S(1)} %get-tuple-element.25.refs_0_.refs_8_), channel_id=1, source_target_pairs={{0,12},{4,8},{8,4},{12,0},{1,13},{5,9},{9,5},{13,1},{2,14},{6,10},... | collective-permute-start | bytes 12296 | tf_op jit(solution)/shard_map/ppermute | solution.py:359
  13.4 0.1 collective-permute-start.1
  13.6 1.8 %collective-permute-start = (f32[8,128]{1,0:T(8,128)S(1)}, f32[8,128]{1,0:T(8,128)S(1)}, u32[]{:S(2)}, u32[]{:S(2)}) collective-permute-start(f32[8,128]{1,0:T(8,128)S(1)} %get-tuple-element.25.refs_0_.refs_8_), channel_id=1, source_target_pairs={{0,4},{4,0},{8,12},{12,8},{1,5},{5,1},{9,13},{13,9},{2,6},{6,2},{1... | collective-permute-start | bytes 12296 | tf_op jit(solution)/shard_map/ppermute | solution.py:359
  15.3 1.7 %collective-permute-start.7 = (bf16[512,128]{1,0:T(8,128)(2,1)S(1)}, bf16[512,128]{1,0:T(8,128)(2,1)S(1)}, u32[]{:S(2)}, u32[]{:S(2)}) collective-permute-start(bf16[512,128]{1,0:T(8,128)(2,1)S(1)} %get-tuple-element.46), channel_id=1, source_target_pairs={{0,8},{4,12},{8,0},{12,4},{1,9},{5,13},{9,1},{13,5},{2,10},{6,14},... | collective-permute-start | bytes 393224 | tf_op jit(solution)/shard_map/ppermute | solution.py:359
  17.0 0.0 collective-permute-done.2.refs_3_.refs_11_
  17.1 1.8 %collective-permute-start.8 = (bf16[512,128]{1,0:T(8,128)(2,1)S(1)}, bf16[512,128]{1,0:T(8,128)(2,1)S(1)}, u32[]{:S(2)}, u32[]{:S(2)}) collective-permute-start(bf16[512,128]{1,0:T(8,128)(2,1)S(1)} %get-tuple-element.47), channel_id=1, source_target_pairs={{0,12},{4,8},{8,4},{12,0},{1,13},{5,9},{9,5},{13,1},{2,14},{6,10},... | collective-permute-start | bytes 393224 | tf_op jit(solution)/shard_map/ppermute | solution.py:359
  18.8 0.2 collective-permute-done.1.refs_2_.refs_10_
  19.1 0.0 collective-permute-done.refs_1_.refs_9_
  19.1 0.0 copy-done
  19.1 0.5 %resume.1 = (bf16[512,128]{1,0:T(8,128)(2,1)S(1)}, bf16[512,128]{1,0:T(8,128)(2,1)S(1)}, bf16[512,128]{1,0:T(8,128)(2,1)S(1)}, bf16[512,128]{1,0:T(8,128)(2,1)S(1)}) custom-call(f32[8,128]{1,0:T(8,128)S(1)} %get-tuple-element.25.refs_0_.refs_8_, f32[8,128]{1,0:T(8,128)S(1)} %collective-permute-done.refs_1_.refs_9_, ...), custom_call_target="tpu_custom_call" | custom-call | flops 67108864 | bytes 2097152 | tf_op jit(solution)/shard_map/resume/pallas_call | solution.py:365
  19.6 0.1 collective-permute-start.3
  19.7 2.4 %collective-permute-start.4 = (bf16[512,128]{1,0:T(8,128)(2,1)S(1)}, bf16[512,128]{1,0:T(8,128)(2,1)S(1)}, u32[]{:S(2)}, u32[]{:S(2)}) collective-permute-start(bf16[512,128]{1,0:T(8,128)(2,1)S(1)} %get-tuple-element.30.refs_6_), channel_id=1, source_target_pairs={{0,8},{4,12},{8,0},{12,4},{1,9},{5,13},{9,1},{13,5},{2,10},{6,14},... | collective-permute-start | bytes 393224 | tf_op jit(solution)/shard_map/ppermute | solution.py:359
  22.0 0.0 collective-permute-done.6.refs_1_
  22.0 2.0 %collective-permute-start.5 = (bf16[512,128]{1,0:T(8,128)(2,1)S(1)}, bf16[512,128]{1,0:T(8,128)(2,1)S(1)}, u32[]{:S(2)}, u32[]{:S(2)}) collective-permute-start(bf16[512,128]{1,0:T(8,128)(2,1)S(1)} %get-tuple-element.31.refs_7_), channel_id=1, source_target_pairs={{0,12},{4,8},{8,4},{12,0},{1,13},{5,9},{9,5},{13,1},{2,14},{6,10},... | collective-permute-start | bytes 393224 | tf_op jit(solution)/shard_map/ppermute | solution.py:359
  24.1 7.9 %intra.1 = (f32[512,2048]{1,0:T(8,128)S(1)}, f32[512,2048]{1,0:T(8,128)S(1)}) custom-call(bf16[8,128]{1,0:T(8,128)(2,1)S(1)} %slice.3.after_ref, f32[32,512]{1,0:T(8,128)S(1)} %get-tuple-element.34.step_ref, f32[32,512]{1,0:T(8,128)S(1)} %get-tuple-element.35.log_ref, f32[1,32]{1,0:T(1,128)S(1)} %get-tuple-element.36.skip_ref, ...), custom_call_target="tpu_custom_call" | custom-call | flops 2147483648 | bytes 16777216 | tf_op jit(solution)/shard_map/intra/pallas_call | solution.py:339
  31.9 0.3 collective-permute-done.7.refs_2_
  32.2 0.0 collective-permute-done.8.refs_3_
  32.2 1.2 %final.1 = bf16[4,512,128]{2,1,0:T(8,128)(2,1)} custom-call(bf16[512,128]{1,0:T(8,128)(2,1)S(1)} %get-tuple-element.44.refs_0_, bf16[512,128]{1,0:T(8,128)(2,1)S(1)} %collective-permute-done.6.refs_1_, bf16[512,128]{1,0:T(8,128)(2,1)S(1)} %collective-permute-done.7.refs_2_, bf16[512,128]{1,0:T(8,128)(2,1)S(1)} %collective-permute-done.8.refs_3_, ...), custom_call_target="tpu_custom_call" | custom-call | flops 67108864 | bytes 2097152 | tf_op jit(solution)/shard_map/final/pallas_call | solution.py:381
  33.4 0.0 collective-permute-done.3.refs_1_
  33.4 4.4 %collective-permute-done.4.refs_2_ = bf16[512,128]{1,0:T(8,128)(2,1)S(1)} collective-permute-done((bf16[512,128]{1,0:T(8,128)(2,1)S(1)}, bf16[512,128]{1,0:T(8,128)(2,1)S(1)}, u32[]{:S(2)}, u32[]{:S(2)}) %collective-permute-start.4) | collective-permute-done | bytes 131104 | tf_op jit(solution)/shard_map/ppermute | solution.py:359
  37.8 0.0 collective-permute-done.5.refs_3_
  37.8 3.9 %norm.1 = bf16[1,512,2048]{2,1,0:T(8,128)(2,1)} custom-call(bf16[512,128]{1,0:T(8,128)(2,1)S(1)} %get-tuple-element.28.refs_0_.refs_4_, bf16[512,128]{1,0:T(8,128)(2,1)S(1)} %collective-permute-done.3.refs_1_, bf16[512,128]{1,0:T(8,128)(2,1)S(1)} %collective-permute-done.4.refs_2_, bf16[512,128]{1,0:T(8,128)(2,1)S(1)} %collective-permute-done.5.refs_3_, ...), custom_call_target="tpu_custom_call" | custom-call | flops 268435456 | bytes 4194304 | tf_op jit(solution)/shard_map/norm/pallas_call | solution.py:414
  (1 shorter events, 0.0 us)
Async XLA Ops:
  0.6 18.4 %copy-start = (bf16[16,32,16,128]{3,2,1,0:T(8,128)(2,1)S(1)}, bf16[16,32,16,128]{3,2,1,0:T(8,128)(2,1)}, u32[]{:S(2)}) copy-start(bf16[16,32,16,128]{3,2,1,0:T(8,128)(2,1)} %param.22) | copy-start | bytes 6291460
  7.8 14.2 %collective-permute-start.6 = (bf16[512,128]{1,0:T(8,128)(2,1)S(1)}, bf16[512,128]{1,0:T(8,128)(2,1)S(1)}, u32[]{:S(2)}, u32[]{:S(2)}) collective-permute-start(bf16[512,128]{1,0:T(8,128)(2,1)S(1)} %get-tuple-element.45), channel_id=1, source_target_pairs={{0,4},{4,0},{8,12},{12,8},{1,5},{5,1},{9,13},{13,9},{2,6},{6,2},{1... | collective-permute-start | bytes 393224 | tf_op jit(solution)/shard_map/ppermute | solution.py:359
  11.0 6.1 %collective-permute-start.2 = (f32[8,128]{1,0:T(8,128)S(1)}, f32[8,128]{1,0:T(8,128)S(1)}, u32[]{:S(2)}, u32[]{:S(2)}) collective-permute-start(f32[8,128]{1,0:T(8,128)S(1)} %get-tuple-element.25.refs_0_.refs_8_), channel_id=1, source_target_pairs={{0,12},{4,8},{8,4},{12,0},{1,13},{5,9},{9,5},{13,1},{2,14},{6,10},... | collective-permute-start | bytes 12296 | tf_op jit(solution)/shard_map/ppermute | solution.py:359
  13.4 5.6 %collective-permute-start.1 = (f32[8,128]{1,0:T(8,128)S(1)}, f32[8,128]{1,0:T(8,128)S(1)}, u32[]{:S(2)}, u32[]{:S(2)}) collective-permute-start(f32[8,128]{1,0:T(8,128)S(1)} %get-tuple-element.25.refs_0_.refs_8_), channel_id=1, source_target_pairs={{0,8},{4,12},{8,0},{12,4},{1,9},{5,13},{9,1},{13,5},{2,10},{6,14},... | collective-permute-start | bytes 12296 | tf_op jit(solution)/shard_map/ppermute | solution.py:359
  13.6 5.5 %collective-permute-start = (f32[8,128]{1,0:T(8,128)S(1)}, f32[8,128]{1,0:T(8,128)S(1)}, u32[]{:S(2)}, u32[]{:S(2)}) collective-permute-start(f32[8,128]{1,0:T(8,128)S(1)} %get-tuple-element.25.refs_0_.refs_8_), channel_id=1, source_target_pairs={{0,4},{4,0},{8,12},{12,8},{1,5},{5,1},{9,13},{13,9},{2,6},{6,2},{1... | collective-permute-start | bytes 12296 | tf_op jit(solution)/shard_map/ppermute | solution.py:359
  15.3 16.8 %collective-permute-start.7 = (bf16[512,128]{1,0:T(8,128)(2,1)S(1)}, bf16[512,128]{1,0:T(8,128)(2,1)S(1)}, u32[]{:S(2)}, u32[]{:S(2)}) collective-permute-start(bf16[512,128]{1,0:T(8,128)(2,1)S(1)} %get-tuple-element.46), channel_id=1, source_target_pairs={{0,8},{4,12},{8,0},{12,4},{1,9},{5,13},{9,1},{13,5},{2,10},{6,14},... | collective-permute-start | bytes 393224 | tf_op jit(solution)/shard_map/ppermute | solution.py:359
  17.1 15.1 %collective-permute-start.8 = (bf16[512,128]{1,0:T(8,128)(2,1)S(1)}, bf16[512,128]{1,0:T(8,128)(2,1)S(1)}, u32[]{:S(2)}, u32[]{:S(2)}) collective-permute-start(bf16[512,128]{1,0:T(8,128)(2,1)S(1)} %get-tuple-element.47), channel_id=1, source_target_pairs={{0,12},{4,8},{8,4},{12,0},{1,13},{5,9},{9,5},{13,1},{2,14},{6,10},... | collective-permute-start | bytes 393224 | tf_op jit(solution)/shard_map/ppermute | solution.py:359
  19.6 13.8 %collective-permute-start.3 = (bf16[512,128]{1,0:T(8,128)(2,1)S(1)}, bf16[512,128]{1,0:T(8,128)(2,1)S(1)}, u32[]{:S(2)}, u32[]{:S(2)}) collective-permute-start(bf16[512,128]{1,0:T(8,128)(2,1)S(1)} %get-tuple-element.29.refs_5_), channel_id=1, source_target_pairs={{0,4},{4,0},{8,12},{12,8},{1,5},{5,1},{9,13},{13,9},{2,6},{6,2},{1... | collective-permute-start | bytes 393224 | tf_op jit(solution)/shard_map/ppermute | solution.py:359
  19.7 18.1 %collective-permute-start.4 = (bf16[512,128]{1,0:T(8,128)(2,1)S(1)}, bf16[512,128]{1,0:T(8,128)(2,1)S(1)}, u32[]{:S(2)}, u32[]{:S(2)}) collective-permute-start(bf16[512,128]{1,0:T(8,128)(2,1)S(1)} %get-tuple-element.30.refs_6_), channel_id=1, source_target_pairs={{0,8},{4,12},{8,0},{12,4},{1,9},{5,13},{9,1},{13,5},{2,10},{6,14},... | collective-permute-start | bytes 393224 | tf_op jit(solution)/shard_map/ppermute | solution.py:359
  22.0 15.7 %collective-permute-start.5 = (bf16[512,128]{1,0:T(8,128)(2,1)S(1)}, bf16[512,128]{1,0:T(8,128)(2,1)S(1)}, u32[]{:S(2)}, u32[]{:S(2)}) collective-permute-start(bf16[512,128]{1,0:T(8,128)(2,1)S(1)} %get-tuple-element.31.refs_7_), channel_id=1, source_target_pairs={{0,12},{4,8},{8,4},{12,0},{1,13},{5,9},{9,5},{13,1},{2,14},{6,10},... | collective-permute-start | bytes 393224 | tf_op jit(solution)/shard_map/ppermute | solution.py:359

commit v4 on v3

--- a/solution.py
+++ b/solution.py
@@ -10,11 +10,12 @@
 HEAD_SIZE = 64
 GROUP_HEADS = 32
 CHUNK = 128
+SPAN = 256
 LANES = 256
 F32 = jnp.float32
 BF16 = jnp.bfloat16
 VMEM = pl.BlockSpec(memory_space=pltpu.VMEM)
-SMEM = pl.BlockSpec(memory_space=pltpu.SMEM)
+HBM = pl.BlockSpec(memory_space=pltpu.HBM)
 
 
 def split3(v):
@@ -30,23 +31,19 @@
     return jnp.sum(jnp.where(eye, row, 0.0), axis=1, keepdims=True)
 
 
-def spread_matrix(heads, lanes):
-    term = lax.broadcasted_iota(jnp.int32, (128, 1), 0)
-    head = term
-    for k in (1, 2):
-        head = jnp.where(term >= k * heads, term - k * heads, head)
-    head = jnp.where(term >= 3 * heads, -1, head)
-    first = head * HEAD_SIZE
-    lane = lax.broadcasted_iota(jnp.int32, (1, lanes), 1)
-    hit = jnp.where(lane >= first, 1.0, 0.0) - jnp.where(lane >= first + HEAD_SIZE, 1.0, 0.0)
-    return jnp.where(head >= 0, hit, 0.0).astype(BF16)
-
-
-def stacked(v):
+def turned(v):
     heads, length = v.shape
-    hi, mid, lo = split3(v)
-    full = jnp.concatenate([hi, mid, lo, jnp.zeros((128 - 3 * heads, length), F32)], axis=0)
-    return full.T.astype(BF16)
+    return jnp.concatenate([v, jnp.zeros((128 - heads, length), F32)], axis=0).T
+
+
+def spread(v, first, lanes):
+    per = 128 // HEAD_SIZE
+    lane = lax.broadcasted_iota(jnp.int32, v.shape, 1)
+    tiles = []
+    for j in range(lanes // 128):
+        head = first + j * per + lax.shift_right_logical(lane, HEAD_SIZE.bit_length() - 1)
+        tiles.append(jnp.take_along_axis(v, head, axis=1))
+    return jnp.concatenate(tiles, axis=1)
 
 
 def scan_steps(raw, bias_row, decay_row, alive_count):
@@ -78,54 +75,55 @@
     return step, jnp.concatenate(parts, axis=1)
 
 
-def state_kernel(*refs, ways, dp_name, loads):
-    sources, refs = refs[:loads], refs[loads:]
+def state_kernel(*refs, ways, dp_name):
+    sources, refs = refs[:12], refs[12:]
     pieces, refs = refs[:ways], refs[ways:]
-    meta_ref, spread_ref, step_ref, log_ref, *refs = refs
-    held, (tail_ref, hold, sems) = refs[:loads], refs[loads:]
-    raw_ref, bias_ref, decay_ref, length_ref, slot_ref, b_ref, x_ref = held[:7]
+    meta_ref, step_ref, log_ref, b_ref, x_ref, c_ref, skip_ref, gain_ref, template_ref, decays_ref = refs[:10]
+    raw_ref, bias_ref, decay_ref, count_ref, hold, sems = refs[10:]
     heads, length = raw_ref.shape
     width = heads * HEAD_SIZE
     chan = HEAD_SIZE // ways
+    targets = [raw_ref, bias_ref, decay_ref, count_ref.at[0:1], count_ref.at[1:2], b_ref, x_ref]
+    targets += [c_ref, skip_ref, gain_ref, template_ref, decays_ref]
     copies = [
         pltpu.make_async_copy(source, target, sems.at[i])
-        for i, (source, target) in enumerate(zip(sources, held))
+        for i, (source, target) in enumerate(zip(sources, targets))
     ]
     for copy in copies:
         copy.start()
-    spread_ref[...] = spread_matrix(heads, width)
-    for copy in copies[:4]:
+    for copy in copies[:5]:
         copy.wait()
-    step, logdecay = scan_steps(raw_ref[...], bias_ref[...], decay_ref[...], length_ref[...])
+    step, logdecay = scan_steps(raw_ref[...], bias_ref[...], decay_ref[...], count_ref[0:1, 0:1])
     step_ref[...] = step
     log_ref[...] = logdecay
     end = logdecay[:, length - 1 :]
-    tail_ref[...] = stacked(jnp.exp(end - logdecay) * step)
-    lane = lax.broadcasted_iota(jnp.int32, (8, 128), 1)
-    eye = lax.broadcasted_iota(jnp.int32, (heads, 128), 0) == lax.broadcasted_iota(
-        jnp.int32, (heads, 128), 1
-    )
-    last = jnp.sum(jnp.where(eye, jnp.exp(end), 0.0), axis=0, keepdims=True)
-    for copy in copies[4:7]:
+    tail = turned(jnp.exp(end - logdecay) * step)
+    for copy in copies[5:7]:
         copy.wait()
-    slot = slot_ref[...].astype(F32)
-    meta_ref[...] = jnp.where(lane == heads, slot, jnp.broadcast_to(last, (8, 128)))
     turned_b = b_ref[...].T
     per = LANES // HEAD_SIZE
     for t in range(width // LANES):
         at = slice(t * LANES, (t + 1) * LANES)
-        scale = jnp.dot(tail_ref[...], spread_ref[:, at], preferred_element_type=F32)
-        moved = (scale * x_ref[:, at].astype(F32)).astype(BF16)
+        moved = (spread(tail, t * per, LANES) * x_ref[:, at].astype(F32)).astype(BF16)
         state = jnp.dot(turned_b, moved, preferred_element_type=F32)
-        turned = state.T.astype(BF16).reshape(per, ways, chan, 128)
+        back = state.T.astype(BF16).reshape(per, ways, chan, 128)
         for d in range(ways):
-            hold[d, t * per * chan : (t + 1) * per * chan, :] = turned[:, d].reshape(per * chan, 128)
+            hold[d, t * per * chan : (t + 1) * per * chan, :] = back[:, d].reshape(per * chan, 128)
     if ways == 1:
         pieces[0][...] = hold[0]
     else:
         me = lax.axis_index(dp_name)
         for k in range(ways):
             pieces[k][...] = hold[me ^ k]
+    lane = lax.broadcasted_iota(jnp.int32, (8, 128), 1)
+    eye = lax.broadcasted_iota(jnp.int32, (heads, 128), 0) == lax.broadcasted_iota(
+        jnp.int32, (heads, 128), 1
+    )
+    last = jnp.sum(jnp.where(eye, jnp.exp(end), 0.0), axis=0, keepdims=True)
+    last = jnp.broadcast_to(last, (8, 128))
+    counts = count_ref[...].astype(F32)
+    last = jnp.where(lane == heads, counts[1:2, 0:1], last)
+    meta_ref[...] = jnp.where(lane == heads + 1, counts[0:1, 0:1], last)
     for copy in copies[7:]:
         copy.wait()
 
@@ -152,76 +150,68 @@
 
 
 def intra_kernel(
-    after_ref,
-    step_ref,
-    log_ref,
-    skip_ref,
-    spread_ref,
-    x_ref,
-    b_ref,
-    c_ref,
-    y_ref,
-    grow_ref,
-    in_ref,
-    out_ref,
-    whole_ref,
-    mix_ref,
-    ends_ref,
+    after_ref, step_ref, log_ref, skip_ref, x_ref, b_ref, c_ref, y_ref, grow_ref, mix_ref
 ):
     heads, length = step_ref.shape
     width = heads * HEAD_SIZE
-    chunks = length // CHUNK
-    causal = lax.broadcasted_iota(jnp.int32, (CHUNK, CHUNK), 0) >= lax.broadcasted_iota(
-        jnp.int32, (CHUNK, CHUNK), 1
+    spans = length // SPAN
+    causal = lax.broadcasted_iota(jnp.int32, (SPAN, SPAN), 0) >= lax.broadcasted_iota(
+        jnp.int32, (SPAN, SPAN), 1
     )
     lane = lax.broadcasted_iota(jnp.int32, (heads, 128), 1)
-    ends = jnp.zeros((heads, 128), F32)
+    rates = jnp.zeros((heads, 128), F32)
     start = jnp.zeros((heads, 1), F32)
-    for c in range(chunks):
-        at = slice(c * CHUNK, (c + 1) * CHUNK)
+    inner, outer, turned_b = [], [], []
+    for i in range(spans):
+        at = slice(i * SPAN, (i + 1) * SPAN)
         logdecay = log_ref[:, at]
-        inside = logdecay - start
-        in_ref[at, :] = stacked(jnp.exp(-inside) * step_ref[:, at])
-        out_ref[at, :] = stacked(jnp.exp(inside))
-        whole_ref[at, :] = stacked(jnp.exp(logdecay))
-        ends = jnp.where(lane == c, jnp.exp(inside[:, CHUNK - 1 :]), ends)
-        start = logdecay[:, CHUNK - 1 :]
+        middle = logdecay[:, SPAN // 2 - 1 : SPAN // 2]
+        end = logdecay[:, SPAN - 1 :]
+        inside = logdecay - middle
+        inner.append(turned(jnp.exp(-inside) * step_ref[:, at]))
+        outer.append(turned(jnp.exp(inside)))
+        for j, v in enumerate((jnp.exp(middle - start), jnp.exp(end - middle), jnp.exp(middle))):
+            rates = jnp.where(lane == 3 * i + j, v, rates)
+        start = end
         gram = lax.dot_general(
             c_ref[at, :], b_ref[at, :], (((1,), (1,)), ((), ())), preferred_element_type=F32
         )
-        mix_ref[at, :CHUNK] = jnp.where(causal, gram, 0.0).astype(BF16)
-        mix_ref[at, CHUNK:] = c_ref[at, :]
-    ends_ref[...] = stacked(ends)
-    skip_row = jnp.concatenate(split3(skip_ref[...]) + (jnp.zeros((1, 128 - 3 * heads), F32),), axis=1)
-    skip_rows = jnp.broadcast_to(skip_row, (8, 128)).astype(BF16)
-
+        mix_ref[at, :] = jnp.where(causal, gram, 0.0).astype(BF16)
+        turned_b.append(b_ref[at, :].T)
+    rates = turned(rates)[: 8 * -(-3 * spans // 8)]
+    eight = jnp.broadcast_to(
+        jnp.concatenate([skip_ref[...], jnp.zeros((1, 128 - heads), F32)], axis=1), (8, 128)
+    )
+
+    per = LANES // HEAD_SIZE
     for t in range(width // LANES):
         at = slice(t * LANES, (t + 1) * LANES)
-        hot = spread_ref[:, at]
-        skip = jnp.dot(skip_rows, hot, preferred_element_type=F32)[0:1]
-        decay = jnp.dot(ends_ref[0:8, :], hot, preferred_element_type=F32)
-        state = jnp.zeros((128, LANES), F32)
-        for c in range(chunks):
-            rows = slice(c * CHUNK, (c + 1) * CHUNK)
+        skip = spread(eight, t * per, LANES)[0:1]
+        rate = spread(rates, t * per, LANES)
+        state = None
+        for i in range(spans):
+            rows = slice(i * SPAN, (i + 1) * SPAN)
+            into, out, whole = (rate[3 * i + j : 3 * i + j + 1] for j in range(3))
             x = x_ref[rows, at].astype(F32)
-            inner = jnp.dot(in_ref[rows, :], hot, preferred_element_type=F32)
-            moved = (x * inner).astype(BF16)
-            both = jnp.concatenate([moved, state.astype(BF16)], axis=0)
-            mixed = jnp.dot(mix_ref[rows, :], both, preferred_element_type=F32)
-            outer = jnp.dot(out_ref[rows, :], hot, preferred_element_type=F32)
-            y_ref[rows, at] = outer * mixed + skip * x
-            grow_ref[rows, at] = jnp.dot(whole_ref[rows, :], hot, preferred_element_type=F32)
-            if c + 1 < chunks:
-                fresh = lax.dot_general(
-                    b_ref[rows, :], moved, (((0,), (0,)), ((), ())), preferred_element_type=F32
+            moved = (x * spread(inner[i], t * per, LANES)).astype(BF16)
+            mixed = jnp.dot(mix_ref[rows, :], moved, preferred_element_type=F32)
+            if state is not None:
+                mixed += jnp.dot(
+                    c_ref[rows, :], (into * state).astype(BF16), preferred_element_type=F32
                 )
-                state = decay[c : c + 1] * (state + fresh)
+            scale = spread(outer[i], t * per, LANES)
+            y_ref[rows, at] = scale * mixed + skip * x
+            grow_ref[rows, at] = scale * whole
+            if i + 1 < spans:
+                fresh = jnp.dot(turned_b[i], moved, preferred_element_type=F32)
+                state = out * (fresh if state is None else into * state + fresh)
 
 
 def norm_kernel(*refs, ways, dp_name, heads, block):
     pieces, refs = refs[:ways], refs[ways:]
-    length_ref, offset_ref, y_ref, grow_ref, c_ref, gain_ref, mixed_ref, hold, done, sems = refs
+    meta_ref, offset_ref, y_ref, grow_ref, c_ref, gain_ref, mixed_ref, hold, scan_ref, done, sems = refs
     chan = HEAD_SIZE // ways
+    width = heads * HEAD_SIZE
     if ways == 1:
         hold[...] = pieces[0][...]
     else:
@@ -230,18 +220,28 @@
             start = pl.multiple_of((me ^ k) * chan, chan)
             for h in range(heads):
                 hold[pl.ds(h * HEAD_SIZE + start, chan), :] = pieces[k][h * chan : (h + 1) * chan, :]
-    position = lax.broadcasted_iota(jnp.int32, (block, 1), 0)
+    position = lax.broadcasted_iota(jnp.int32, (block, 1), 0).astype(F32)
+    length, offset = meta_ref[0:1, heads + 1 : heads + 2], offset_ref[...].astype(F32)
     copies = []
     for i in range(y_ref.shape[0] // block):
         rows = slice(i * block, (i + 1) * block)
-        carried = lax.dot_general(
-            c_ref[rows, :], hold[...], (((1,), (1,)), ((), ())), preferred_element_type=F32
-        )
-        scan = y_ref[rows, :] + grow_ref[rows, :] * carried
-        meansq = jnp.mean(scan * scan, axis=1, keepdims=True)
-        keep = (position + i * block < length_ref[...]) & (position + i * block >= offset_ref[...])
+        squares = jnp.zeros((block, 128), F32)
+        for t in range(width // LANES):
+            at = slice(t * LANES, (t + 1) * LANES)
+            carried = lax.dot_general(
+                c_ref[rows, :], hold[at, :], (((1,), (1,)), ((), ())), preferred_element_type=F32
+            )
+            scan = y_ref[rows, at] + grow_ref[rows, at] * carried
+            scan_ref[rows, at] = scan
+            for j in range(LANES // 128):
+                part = scan[:, j * 128 : (j + 1) * 128]
+                squares += part * part
+        meansq = jnp.sum(squares, axis=1, keepdims=True) * (1.0 / width)
+        keep = (position + i * block < length) & (position + i * block >= offset)
         factor = jnp.where(keep, lax.rsqrt(meansq + 1e-05), 0.0)
-        done[rows, :] = (scan * factor * gain_ref[...]).astype(BF16)
+        for t in range(width // LANES):
+            at = slice(t * LANES, (t + 1) * LANES)
+            done[rows, at] = (scan_ref[rows, at] * factor * gain_ref[:, at]).astype(BF16)
         copy = pltpu.make_async_copy(done.at[rows, :], mixed_ref.at[0, rows, :], sems.at[i])
         copy.start()
         copies.append(copy)
@@ -306,25 +306,23 @@
         output_proj[0],
         skip_gain[None],
         norm_gain[None],
-        row_offsets[None],
         template_state.reshape(-1, state),
         slot_decay,
     ]
-    shape_of = lambda v: jax.ShapeDtypeStruct(v.shape, v.dtype)
+    like = lambda v: jax.ShapeDtypeStruct(v.shape, v.dtype)
     outs = pl.pallas_call(
-        functools.partial(state_kernel, ways=ways, dp_name="dp", loads=len(loaded)),
+        functools.partial(state_kernel, ways=ways, dp_name="dp"),
         out_shape=[piece] * ways
-        + [
-            jax.ShapeDtypeStruct((8, 128), F32),
-            jax.ShapeDtypeStruct((128, width), BF16),
-            jax.ShapeDtypeStruct((heads, length), F32),
-            jax.ShapeDtypeStruct((heads, length), F32),
-        ]
-        + [shape_of(v) for v in loaded],
-        in_specs=[pl.BlockSpec(memory_space=pltpu.HBM)] * len(loaded),
-        out_specs=[VMEM] * (ways + 4 + len(loaded)),
+        + [jax.ShapeDtypeStruct((8, 128), F32)]
+        + [jax.ShapeDtypeStruct((heads, length), F32)] * 2
+        + [like(v) for v in loaded[5:]],
+        in_specs=[HBM] * len(loaded),
+        out_specs=[VMEM] * (ways + 3 + len(loaded[5:])),
         scratch_shapes=[
-            pltpu.VMEM((length, 128), BF16),
+            pltpu.VMEM((heads, length), F32),
+            pltpu.VMEM((1, heads), F32),
+            pltpu.VMEM((1, heads), F32),
+            pltpu.VMEM((2, 1), jnp.int32),
             pltpu.VMEM((ways, rows, state), BF16),
             pltpu.SemaphoreType.DMA((len(loaded),)),
         ],
@@ -332,26 +330,20 @@
         cost_estimate=cost(2 * length * width * 256, 3 << 20),
         name="state",
     )(*[pinned(v) for v in loaded])
-    local_parts, (meta, spread, step, logdecay, *held) = outs[:ways], outs[ways:]
-    _, _, _, alive, _, b, x, c, skip, gain, offset, template, decays = held
+    local_parts = outs[:ways]
+    meta, step, logdecay, b, x, c, skip, gain, template, decays = outs[ways:]
 
     def intra(after):
         return pl.pallas_call(
             intra_kernel,
             out_shape=[jax.ShapeDtypeStruct((length, width), F32)] * 2,
-            in_specs=[VMEM] * 8,
+            in_specs=[VMEM] * 7,
             out_specs=[VMEM] * 2,
-            scratch_shapes=[
-                pltpu.VMEM((length, 128), BF16),
-                pltpu.VMEM((length, 128), BF16),
-                pltpu.VMEM((length, 128), BF16),
-                pltpu.VMEM((length, 2 * CHUNK), BF16),
-                pltpu.VMEM((128, 128), BF16),
-            ],
+            scratch_shapes=[pltpu.VMEM((length, SPAN), BF16)],
             compiler_params=params,
             cost_estimate=cost(2 * length * width * 1024, 16 << 20),
             name="intra",
-        )(after, step, logdecay, skip, spread, x, b, c)
+        )(after, step, logdecay, skip, x, b, c)
 
     if direct:
 
@@ -415,16 +407,17 @@
         functools.partial(norm_kernel, ways=ways, dp_name="dp", heads=heads, block=block),
         out_shape=jax.ShapeDtypeStruct((1, length, width), BF16),
         in_specs=[VMEM] * (ways + 6),
-        out_specs=pl.BlockSpec(memory_space=pltpu.HBM),
+        out_specs=HBM,
         scratch_shapes=[
             pltpu.VMEM((heads * HEAD_SIZE, state), BF16),
+            pltpu.VMEM((length, width), F32),
             pltpu.VMEM((length, width), BF16),
             pltpu.SemaphoreType.DMA((length // block,)),
         ],
         compiler_params=params,
         cost_estimate=cost(2 * length * width * 128, 4 << 20),
         name="norm",
-    )(*arrived, alive, offset, y, grow, c, gain)
+    )(*arrived, meta, row_offsets[None], y, grow, c, gain)
     return (mixed, new_states)
 
 

time: 41.9 us -> 38.7 us (0.924)
  Pallas kernels: 18.6 us -> 11.8 us
  waiting for transfers between devices: 4.89 us -> 9.3 us
  starting transfers between devices: 15.4 us -> 14.6 us
    ppermute x9, waiting for transfers between devices: 4.89 us -> 9.3 us  [swap(): return lax.ppermute(v, 'dp', [(i, i ^ k) for i in range(dp)])]
    pallas_call x1, Pallas kernels: 7.86 us -> 3.6 us  [intra(): pl.pallas_call(intra_kernel, out_shape=[jax.ShapeDtypeStruct((length, wid...]
    pallas_call x1, Pallas kernels: 3.95 us -> 2.65 us  [local(): pl.pallas_call(functools.partial(norm_kernel, ways=ways, dp_name='dp', he...]
    pallas_call x1, Pallas kernels: 5.1 us -> 3.81 us  [local(): pl.pallas_call(functools.partial(state_kernel, ways=ways, dp_name='dp'),...]
    ppermute x9, starting transfers between devices: 15.4 us -> 14.6 us  [swap(): return lax.ppermute(v, 'dp', [(i, i ^ k) for i in range(dp)])]
  transfers between devices with their start and end apart: 9 -> 9, of which waited for: 3 -> 3; matrix products, arithmetic and copies ran while one was open for 0% -> 0% of each run, Pallas kernels for 23% -> 14%
where the time goes in v4:
time: 38.7 us; the launch traced here: 38.5 us
  starting transfers between devices  14.6 us (38%)
  Pallas kernels  11.8 us (30%)
  waiting for transfers between devices  9.3 us (24%)
  between operations  2.78 us (7%)
    ppermute x9, starting transfers between devices, swap(): return lax.ppermute(v, 'dp', [(i, i ^ k) for i in range(dp)])  14.6 us
    ppermute x9, waiting for transfers between devices, swap(): return lax.ppermute(v, 'dp', [(i, i ^ k) for i in range(dp)])  9.3 us
    pallas_call x1, Pallas kernels, local(): pl.pallas_call(functools.partial(state_kernel, ways=ways, dp_name='dp'),...  3.81 us
    pallas_call x1, Pallas kernels, intra(): pl.pallas_call(intra_kernel, out_shape=[jax.ShapeDtypeStruct((length, wid...  3.6 us
    pallas_call x1, Pallas kernels, local(): pl.pallas_call(functools.partial(norm_kernel, ways=ways, dp_name='dp', he...  2.65 us
    pallas_call x1, Pallas kernels, local(): pl.pallas_call(functools.partial(final_kernel, ways=dp, dp_name='dp', hea...  1.23 us
  transfers between devices with their start and end apart: 9, of which 3 were waited for; matrix products, arithmetic and copies ran while one was open for 0% of the time, Pallas kernels for 14%

profile of v4, /device:TPU:0, one launch (start us, length us, event | category | flops | bytes accessed | tf_op | source)
XLA Modules:
  0.0 38.5 jit_solution(14389680761020868450)
XLA Ops:
  0.6 0.0 copy-start
  2.1 3.8 %state.1 = (bf16[512,128]{1,0:T(8,128)(2,1)S(1)}, bf16[512,128]{1,0:T(8,128)(2,1)S(1)}, bf16[512,128]{1,0:T(8,128)(2,1)S(1)}, bf16[512,128]{1,0:T(8,128)(2,1)S(1...) custom-call(f32[32,512]{1,0:T(8,128)} %bitcast.23, ...), custom_call_target="tpu_custom_call" | custom-call | flops 536870912 | bytes 3145728 | tf_op jit(solution)/shard_map/state/pallas_call | solution.py:313
  5.9 3.1 %collective-permute-start.6 = (bf16[512,128]{1,0:T(8,128)(2,1)S(1)}, bf16[512,128]{1,0:T(8,128)(2,1)S(1)}, u32[]{:S(2)}, u32[]{:S(2)}) collective-permute-start(bf16[512,128]{1,0:T(8,128)(2,1)S(1)} %get-tuple-element.39), channel_id=1, source_target_pairs={{0,4},{4,0},{8,12},{12,8},{1,5},{5,1},{9,13},{13,9},{2,6},{6,2},{1... | collective-permute-start | bytes 393224 | tf_op jit(solution)/shard_map/ppermute | solution.py:351
  9.0 0.1 collective-permute-start
  9.1 3.0 %collective-permute-start.1 = (f32[8,128]{1,0:T(8,128)S(1)}, f32[8,128]{1,0:T(8,128)S(1)}, u32[]{:S(2)}, u32[]{:S(2)}) collective-permute-start(f32[8,128]{1,0:T(8,128)S(1)} %get-tuple-element.22.refs_0_.refs_4_.refs_8_), channel_id=1, source_target_pairs={{0,8},{4,12},{8,0},{12,4},{1,9},{5,13},{9,1},{13,5},{2,10},{6,14},... | collective-permute-start | bytes 12296 | tf_op jit(solution)/shard_map/ppermute | solution.py:351
  12.1 1.3 %collective-permute-start.2 = (f32[8,128]{1,0:T(8,128)S(1)}, f32[8,128]{1,0:T(8,128)S(1)}, u32[]{:S(2)}, u32[]{:S(2)}) collective-permute-start(f32[8,128]{1,0:T(8,128)S(1)} %get-tuple-element.22.refs_0_.refs_4_.refs_8_), channel_id=1, source_target_pairs={{0,12},{4,8},{8,4},{12,0},{1,13},{5,9},{9,5},{13,1},{2,14},{6,10},... | collective-permute-start | bytes 12296 | tf_op jit(solution)/shard_map/ppermute | solution.py:351
  13.4 1.7 %collective-permute-start.7 = (bf16[512,128]{1,0:T(8,128)(2,1)S(1)}, bf16[512,128]{1,0:T(8,128)(2,1)S(1)}, u32[]{:S(2)}, u32[]{:S(2)}) collective-permute-start(bf16[512,128]{1,0:T(8,128)(2,1)S(1)} %get-tuple-element.40), channel_id=1, source_target_pairs={{0,8},{4,12},{8,0},{12,4},{1,9},{5,13},{9,1},{13,5},{2,10},{6,14},... | collective-permute-start | bytes 393224 | tf_op jit(solution)/shard_map/ppermute | solution.py:351
  15.8 0.0 collective-permute-done.refs_1_.refs_9_
  15.8 1.0 %collective-permute-start.8 = (bf16[512,128]{1,0:T(8,128)(2,1)S(1)}, bf16[512,128]{1,0:T(8,128)(2,1)S(1)}, u32[]{:S(2)}, u32[]{:S(2)}) collective-permute-start(bf16[512,128]{1,0:T(8,128)(2,1)S(1)} %get-tuple-element.41), channel_id=1, source_target_pairs={{0,12},{4,8},{8,4},{12,0},{1,13},{5,9},{9,5},{13,1},{2,14},{6,10},... | collective-permute-start | bytes 393224 | tf_op jit(solution)/shard_map/ppermute | solution.py:351
  16.7 0.0 collective-permute-done.1.refs_2_.refs_10_
  16.7 0.7 %collective-permute-done.2.refs_3_.refs_11_ = f32[8,128]{1,0:T(8,128)S(1)} collective-permute-done((f32[8,128]{1,0:T(8,128)S(1)}, f32[8,128]{1,0:T(8,128)S(1)}, u32[]{:S(2)}, u32[]{:S(2)}) %collective-permute-start.2) | collective-permute-done | bytes 4128 | tf_op jit(solution)/shard_map/ppermute | solution.py:351
  17.5 0.0 copy-done
  17.5 0.5 %resume.1 = (bf16[512,128]{1,0:T(8,128)(2,1)S(1)}, bf16[512,128]{1,0:T(8,128)(2,1)S(1)}, bf16[512,128]{1,0:T(8,128)(2,1)S(1)}, bf16[512,128]{1,0:T(8,128)(2,1)S(1)}) custom-call(f32[8,128]{1,0:T(8,128)S(1)} %get-tuple-element.22.refs_0_.refs_4_.refs_8_, f32[8,128]{1,0:T(8,128)S(1)} %collective-permute-done.refs_1_.refs_9_, ...), custom_call_target="tpu_custom_call" | custom-call | flops 67108864 | bytes 2097152 | tf_op jit(solution)/shard_map/resume/pallas_call | solution.py:357
  18.0 0.3 collective-permute-start.3
  18.3 2.5 %collective-permute-start.4 = (bf16[512,128]{1,0:T(8,128)(2,1)S(1)}, bf16[512,128]{1,0:T(8,128)(2,1)S(1)}, u32[]{:S(2)}, u32[]{:S(2)}) collective-permute-start(bf16[512,128]{1,0:T(8,128)(2,1)S(1)} %get-tuple-element.27.refs_6_), channel_id=1, source_target_pairs={{0,8},{4,12},{8,0},{12,4},{1,9},{5,13},{9,1},{13,5},{2,10},{6,14},... | collective-permute-start | bytes 393224 | tf_op jit(solution)/shard_map/ppermute | solution.py:351
  20.8 0.0 collective-permute-done.6.refs_1_
  20.8 1.6 %collective-permute-start.5 = (bf16[512,128]{1,0:T(8,128)(2,1)S(1)}, bf16[512,128]{1,0:T(8,128)(2,1)S(1)}, u32[]{:S(2)}, u32[]{:S(2)}) collective-permute-start(bf16[512,128]{1,0:T(8,128)(2,1)S(1)} %get-tuple-element.28.refs_7_), channel_id=1, source_target_pairs={{0,12},{4,8},{8,4},{12,0},{1,13},{5,9},{9,5},{13,1},{2,14},{6,10},... | collective-permute-start | bytes 393224 | tf_op jit(solution)/shard_map/ppermute | solution.py:351
  22.4 3.6 %intra.1 = (f32[512,2048]{1,0:T(8,128)S(1)}, f32[512,2048]{1,0:T(8,128)S(1)}) custom-call(bf16[8,128]{1,0:T(8,128)(2,1)S(1)} %slice.3.after_ref, f32[32,512]{1,0:T(8,128)S(1)} %get-tuple-element.29.step_ref, f32[32,512]{1,0:T(8,128)S(1)} %get-tuple-element.30.log_ref, f32[1,32]{1,0:T(1,128)S(1)} %get-tuple-element.31.skip_ref, ...), custom_call_target="tpu_custom_call" | custom-call | flops 2147483648 | bytes 16777216 | tf_op jit(solution)/shard_map/intra/pallas_call | solution.py:337
  26.1 0.8 %collective-permute-done.7.refs_2_ = bf16[512,128]{1,0:T(8,128)(2,1)S(1)} collective-permute-done((bf16[512,128]{1,0:T(8,128)(2,1)S(1)}, bf16[512,128]{1,0:T(8,128)(2,1)S(1)}, u32[]{:S(2)}, u32[]{:S(2)}) %collective-permute-start.7) | collective-permute-done | bytes 131104 | tf_op jit(solution)/shard_map/ppermute | solution.py:351
  26.9 0.0 collective-permute-done.8.refs_3_
  26.9 1.2 %final.1 = bf16[4,512,128]{2,1,0:T(8,128)(2,1)} custom-call(bf16[512,128]{1,0:T(8,128)(2,1)S(1)} %get-tuple-element.38.refs_0_, bf16[512,128]{1,0:T(8,128)(2,1)S(1)} %collective-permute-done.6.refs_1_, bf16[512,128]{1,0:T(8,128)(2,1)S(1)} %collective-permute-done.7.refs_2_, bf16[512,128]{1,0:T(8,128)(2,1)S(1)} %collective-permute-done.8.refs_3_, ...), custom_call_target="tpu_custom_call" | custom-call | flops 67108864 | bytes 2097152 | tf_op jit(solution)/shard_map/final/pallas_call | solution.py:373
  28.1 0.0 collective-permute-done.3.refs_1_
  28.1 7.8 %collective-permute-done.4.refs_2_ = bf16[512,128]{1,0:T(8,128)(2,1)S(1)} collective-permute-done((bf16[512,128]{1,0:T(8,128)(2,1)S(1)}, bf16[512,128]{1,0:T(8,128)(2,1)S(1)}, u32[]{:S(2)}, u32[]{:S(2)}) %collective-permute-start.4) | collective-permute-done | bytes 131104 | tf_op jit(solution)/shard_map/ppermute | solution.py:351
  35.9 0.0 collective-permute-done.5.refs_3_
  35.9 2.7 %norm.1 = bf16[1,512,2048]{2,1,0:T(8,128)(2,1)} custom-call(bf16[512,128]{1,0:T(8,128)(2,1)S(1)} %get-tuple-element.25.refs_0_.refs_4_, bf16[512,128]{1,0:T(8,128)(2,1)S(1)} %collective-permute-done.3.refs_1_, bf16[512,128]{1,0:T(8,128)(2,1)S(1)} %collective-permute-done.4.refs_2_, bf16[512,128]{1,0:T(8,128)(2,1)S(1)} %collective-permute-done.5.refs_3_, ...), custom_call_target="tpu_custom_call" | custom-call | flops 268435456 | bytes 4194304 | tf_op jit(solution)/shard_map/norm/pallas_call | solution.py:406
  (1 shorter events, 0.0 us)
Async XLA Ops:
  0.6 16.8 %copy-start = (bf16[16,32,16,128]{3,2,1,0:T(8,128)(2,1)S(1)}, bf16[16,32,16,128]{3,2,1,0:T(8,128)(2,1)}, u32[]{:S(2)}) copy-start(bf16[16,32,16,128]{3,2,1,0:T(8,128)(2,1)} %param.22) | copy-start | bytes 6291460
  5.9 14.9 %collective-permute-start.6 = (bf16[512,128]{1,0:T(8,128)(2,1)S(1)}, bf16[512,128]{1,0:T(8,128)(2,1)S(1)}, u32[]{:S(2)}, u32[]{:S(2)}) collective-permute-start(bf16[512,128]{1,0:T(8,128)(2,1)S(1)} %get-tuple-element.39), channel_id=1, source_target_pairs={{0,4},{4,0},{8,12},{12,8},{1,5},{5,1},{9,13},{13,9},{2,6},{6,2},{1... | collective-permute-start | bytes 393224 | tf_op jit(solution)/shard_map/ppermute | solution.py:351
  9.0 6.8 %collective-permute-start = (f32[8,128]{1,0:T(8,128)S(1)}, f32[8,128]{1,0:T(8,128)S(1)}, u32[]{:S(2)}, u32[]{:S(2)}) collective-permute-start(f32[8,128]{1,0:T(8,128)S(1)} %get-tuple-element.22.refs_0_.refs_4_.refs_8_), channel_id=1, source_target_pairs={{0,4},{4,0},{8,12},{12,8},{1,5},{5,1},{9,13},{13,9},{2,6},{6,2},{1... | collective-permute-start | bytes 12296 | tf_op jit(solution)/shard_map/ppermute | solution.py:351
  9.1 7.7 %collective-permute-start.1 = (f32[8,128]{1,0:T(8,128)S(1)}, f32[8,128]{1,0:T(8,128)S(1)}, u32[]{:S(2)}, u32[]{:S(2)}) collective-permute-start(f32[8,128]{1,0:T(8,128)S(1)} %get-tuple-element.22.refs_0_.refs_4_.refs_8_), channel_id=1, source_target_pairs={{0,8},{4,12},{8,0},{12,4},{1,9},{5,13},{9,1},{13,5},{2,10},{6,14},... | collective-permute-start | bytes 12296 | tf_op jit(solution)/shard_map/ppermute | solution.py:351
  12.1 5.4 %collective-permute-start.2 = (f32[8,128]{1,0:T(8,128)S(1)}, f32[8,128]{1,0:T(8,128)S(1)}, u32[]{:S(2)}, u32[]{:S(2)}) collective-permute-start(f32[8,128]{1,0:T(8,128)S(1)} %get-tuple-element.22.refs_0_.refs_4_.refs_8_), channel_id=1, source_target_pairs={{0,12},{4,8},{8,4},{12,0},{1,13},{5,9},{9,5},{13,1},{2,14},{6,10},... | collective-permute-start | bytes 12296 | tf_op jit(solution)/shard_map/ppermute | solution.py:351
  13.4 13.5 %collective-permute-start.7 = (bf16[512,128]{1,0:T(8,128)(2,1)S(1)}, bf16[512,128]{1,0:T(8,128)(2,1)S(1)}, u32[]{:S(2)}, u32[]{:S(2)}) collective-permute-start(bf16[512,128]{1,0:T(8,128)(2,1)S(1)} %get-tuple-element.40), channel_id=1, source_target_pairs={{0,8},{4,12},{8,0},{12,4},{1,9},{5,13},{9,1},{13,5},{2,10},{6,14},... | collective-permute-start | bytes 393224 | tf_op jit(solution)/shard_map/ppermute | solution.py:351
  15.8 11.1 %collective-permute-start.8 = (bf16[512,128]{1,0:T(8,128)(2,1)S(1)}, bf16[512,128]{1,0:T(8,128)(2,1)S(1)}, u32[]{:S(2)}, u32[]{:S(2)}) collective-permute-start(bf16[512,128]{1,0:T(8,128)(2,1)S(1)} %get-tuple-element.41), channel_id=1, source_target_pairs={{0,12},{4,8},{8,4},{12,0},{1,13},{5,9},{9,5},{13,1},{2,14},{6,10},... | collective-permute-start | bytes 393224 | tf_op jit(solution)/shard_map/ppermute | solution.py:351
  18.0 10.1 %collective-permute-start.3 = (bf16[512,128]{1,0:T(8,128)(2,1)S(1)}, bf16[512,128]{1,0:T(8,128)(2,1)S(1)}, u32[]{:S(2)}, u32[]{:S(2)}) collective-permute-start(bf16[512,128]{1,0:T(8,128)(2,1)S(1)} %get-tuple-element.26.refs_5_), channel_id=1, source_target_pairs={{0,4},{4,0},{8,12},{12,8},{1,5},{5,1},{9,13},{13,9},{2,6},{6,2},{1... | collective-permute-start | bytes 393224 | tf_op jit(solution)/shard_map/ppermute | solution.py:351
  18.3 17.5 %collective-permute-start.4 = (bf16[512,128]{1,0:T(8,128)(2,1)S(1)}, bf16[512,128]{1,0:T(8,128)(2,1)S(1)}, u32[]{:S(2)}, u32[]{:S(2)}) collective-permute-start(bf16[512,128]{1,0:T(8,128)(2,1)S(1)} %get-tuple-element.27.refs_6_), channel_id=1, source_target_pairs={{0,8},{4,12},{8,0},{12,4},{1,9},{5,13},{9,1},{13,5},{2,10},{6,14},... | collective-permute-start | bytes 393224 | tf_op jit(solution)/shard_map/ppermute | solution.py:351
  20.8 15.0 %collective-permute-start.5 = (bf16[512,128]{1,0:T(8,128)(2,1)S(1)}, bf16[512,128]{1,0:T(8,128)(2,1)S(1)}, u32[]{:S(2)}, u32[]{:S(2)}) collective-permute-start(bf16[512,128]{1,0:T(8,128)(2,1)S(1)} %get-tuple-element.28.refs_7_), channel_id=1, source_target_pairs={{0,12},{4,8},{8,4},{12,0},{1,13},{5,9},{9,5},{13,1},{2,14},{6,10},... | collective-permute-start | bytes 393224 | tf_op jit(solution)/shard_map/ppermute | solution.py:351
